TPU v7x, 128 devices: a whole 4x4x4 slice. The times are simulated.
128 devices in a mesh: bx: 16 (over y, z), by: 8 (over x, core).
Axes of the slice: x: 4, y: 4, z: 4, core: 2. Of those that a mesh axis runs over, the one named last changes fastest.
Arguments:
- normals: float32 [3, 524288], P(None, ('bx', 'by')), may hold values from -60 to 60
- owners: int32 [524288, 1], P(('bx', 'by')), may hold values from 0 to 127; in each aligned block of 4096 rows (0 to 4095, 4096 to 8191, ...) at most 64 rows name the same one
- cells: int32 [524288], P(('bx', 'by')), may hold values from 0 to 262143
- levels: int32 [16, 8], P('bx', 'by'), may hold values from 0 to 3
- rows_inverse: float32 [256, 256], replicated, may hold values from 0 to 0.25
- columns_inverse: float32 [512, 512], replicated, may hold values from 0 to 0.25
- depth_inverse: float32 [256, 256], replicated, may hold values from 0 to 0.25
Outputs:
- iterate: float32 [256, 512, 256], P('bx', 'by')
- implicit: float32 [524288], P(('bx', 'by'))
Inputs may be any that keep to these rules, and one draw needn't show every extreme that they name: `owners`: A brick's number is its index along bx times the number of devices along by plus its index along by. Among the 4096 points of one device at most 64 name one brick, and in every draw some brick is named by exactly 64 of them.
All inputs are finite; a program needn't handle non-finite values.
Results may differ from a plain program's by a relative error of at most 0.0001.
Values sent between devices are 32-bit elements; how exact they have to be, the bound alone decides.
A program may use at most 320 MiB of HBM per device.

v0:
```python
import jax
import jax.numpy as jnp
from jax import lax
from jax.sharding import PartitionSpec as P

CX = 16
CY = 64
NZ = 256
ITERS = 4


screen_base = 1.0


def padded(shard, sides, width):
    for axis, dim in sides:
        peers, length = (lax.axis_size(axis), shard.shape[dim])
        up = [(i, (i + 1) % peers) for i in range(peers - 1)]
        down = [(j, i) for i, j in up]
        last = lax.slice_in_dim(shard, length - width, length, axis=dim)
        initial = lax.slice_in_dim(shard, 0, width, axis=dim)
        before = lax.ppermute(last, axis, up)
        after = lax.ppermute(initial, axis, down)
        shard = jnp.concatenate([before, shard, after], axis=dim)
    return shard


def remainder_of(iterate, source, screening):
    extended = padded(iterate, (("bx", 0), ("by", 1)), 1)
    z_padded = jnp.pad(iterate, ((0, 0), (0, 0), (1, 1)))
    beside = extended[2:, 1:-1] + extended[:-2, 1:-1]
    beside = beside + extended[1:-1, 2:] + extended[1:-1, :-2]
    beside = beside + z_padded[:, :, 2:] + z_padded[:, :, :-2]
    return source - ((6.0 + screening) * iterate - beside)


def sweep_first(remainder, matrix):
    highest = lax.Precision.HIGHEST
    lines = lax.all_to_all(remainder, "bx", split_axis=1, concat_axis=0, tiled=True)
    product = jnp.einsum("ab,bjk->ajk", matrix, lines, precision=highest)
    return lax.all_to_all(product, "bx", split_axis=0, concat_axis=1, tiled=True)


def sweep_second(remainder, matrix):
    highest = lax.Precision.HIGHEST
    lines = lax.all_to_all(remainder, "by", split_axis=0, concat_axis=1, tiled=True)
    product = jnp.einsum("ab,ibk->iak", matrix, lines, precision=highest)
    return lax.all_to_all(product, "by", split_axis=1, concat_axis=0, tiled=True)


def local(normals, owners, cells, levels, rows_inverse, columns_inverse, depth_inverse):
    first_count = lax.axis_size("bx")
    second_count = lax.axis_size("by")
    bricks = first_count * second_count
    point_count = cells.shape[0]
    capacity = 2 * point_count // bricks
    brick_cells = CX * CY * NZ
    target = owners[:, 0]
    onehot = (target[:, None] == jnp.arange(bricks, dtype=jnp.int32)[None, :]).astype(jnp.int32)
    ranking = jnp.sum(onehot * (jnp.cumsum(onehot, axis=0) - 1), axis=1)
    slot_index = target * capacity + ranking
    send_normals = jnp.zeros((3, bricks * capacity), jnp.float32).at[:, slot_index].set(normals)
    send_cells = jnp.zeros((bricks * capacity,), jnp.int32).at[slot_index].set(cells)
    arrived_normals, arrived_cells = (
        lax.all_to_all(
            send_normals.reshape(3, bricks, capacity),
            ("bx", "by"),
            split_axis=1,
            concat_axis=1,
            tiled=True,
        ),
        lax.all_to_all(
            send_cells.reshape(1, bricks, capacity),
            ("bx", "by"),
            split_axis=1,
            concat_axis=1,
            tiled=True,
        ),
    )
    flat_cells = arrived_cells.reshape(-1)
    vector_field = (
        jnp.zeros((3, brick_cells), jnp.float32)
        .at[:, flat_cells]
        .add(arrived_normals.reshape(3, -1))
    )
    vector_field = vector_field.reshape(3, CX, CY, NZ)
    stretched = padded(vector_field, (("bx", 1), ("by", 2)), 1)
    z_padded = jnp.pad(vector_field[2], ((0, 0), (0, 0), (1, 1)))
    source = -0.5 * (
        stretched[0, 2:, 1:-1]
        - stretched[0, :-2, 1:-1]
        + (stretched[1, 1:-1, 2:] - stretched[1, 1:-1, :-2])
        + (z_padded[:, :, 2:] - z_padded[:, :, :-2])
    )
    screening = screen_base * (1.0 + levels[0, 0].astype(jnp.float32))
    highest = lax.Precision.HIGHEST
    iterate = jnp.zeros((CX, CY, NZ), jnp.float32)
    for iteration in range(ITERS):
        remainder = remainder_of(iterate, source, screening)
        iterate = iterate + sweep_first(remainder, rows_inverse)
        remainder = remainder_of(iterate, source, screening)
        iterate = iterate + sweep_second(remainder, columns_inverse)
        remainder = remainder_of(iterate, source, screening)
        iterate = iterate + jnp.einsum("ab,ijb->ija", depth_inverse, remainder, precision=highest)
    sampled = iterate.reshape(-1)[flat_cells]
    returned = lax.all_to_all(
        sampled.reshape(1, bricks, capacity), ("bx", "by"), split_axis=1, concat_axis=1, tiled=True
    )
    implicit = returned.reshape(-1)[slot_index]
    return (iterate, implicit)


def solution(mesh):
    placed = (
        P(None, ("bx", "by")),
        P(("bx", "by"), None),
        P(("bx", "by")),
        P("bx", "by"),
        P(),
        P(),
        P(),
    )
    return jax.shard_map(
        local,
        mesh=mesh,
        in_specs=placed,
        out_specs=(P("bx", "by", None), P(("bx", "by"))),
        check_vma=False,
    )
```

profile of v0, /device:TPU:1, one launch (start us, length us, event | category | flops | bytes accessed | tf_op | source)
XLA Modules:
  0.0 1116.9 jit_solution(1230370783894139399)
XLA Ops:
  8.2 15.7 %scatter_custom_fusion = s32[8192]{0:T(1024)S(1)} fusion(s32[4096]{0:T(1024)S(1)} %bitcast.183, s32[4096]{0:T(1024)} %param.9, s32[]{:T(128)} %constant.9.clone.1), kind=kCustom, calls=%fused_computation.330 | custom fusion | bytes 33280 | tf_op jit(solution)/shard_map/scatter | solution.py:63
  24.6 11.5 %all-to-all-start = ((s32[1,128,64]{2,0,1:T(1,128)}), s32[1,128,64]{2,0,1:T(1,128)S(1)}, u32[]{:S(2)}, u32[]{:S(2)}) async-start(s32[1,128,64]{2,0,1:T(1,128)} %bitcast.7), calls=%async_computation | async-start | bytes 131072 | tf_op jit(solution)/shard_map/all_to_all | solution.py:72
  38.1 13.1 %scatter_custom_fusion.1 = f32[3,8192]{0,1:T(8,128)} fusion(s32[4096]{0:T(1024)S(1)} %bitcast.184, f32[4096,3]{1,0:T(8,128)} %copy.120, f32[]{:T(128)} %constant.8.clone.1), kind=kCustom, calls=%fused_computation.14 | custom fusion | bytes 98816 | tf_op jit(solution)/shard_map/scatter | solution.py:62
  55.1 10.3 all-to-all-start.1
  67.1 5.9 sort
  79.9 160.5 %scatter_custom_fusion.2 = f32[3,262144]{0,1:T(8,128)} fusion(s32[8192]{0:T(1024)S(1)} %get-tuple-element.2, f32[]{:T(128)} %constant.8.clone.1, f32[8192,3]{1,0:T(8,128)} %copy.123, s32[8192]{0:T(1024)S(1)} %broadcast_clamp_fusion.1), kind=kCustom, calls=%fused_computation.7 | custom fusion | flops 24576 | bytes 3146240 | tf_op jit(solution)/shard_map/scatter-add | solution.py:84
  240.5 77.2 %copy.180 = f32[3,16,64,256]{3,2,1,0:T(8,128)} copy(f32[3,16,64,256]{0,3,2,1:T(8,128)} %bitcast.12) | data formatting | bytes 6291456 | tf_op jit(solution)/shard_map/reshape | solution.py:86
  345.7 74.8 %slice_reduce_fusion = f32[262144]{0:T(1024)S(1)} fusion(f32[3,262144]{0,1:T(8,128)} %scatter_custom_fusion.2), kind=kLoop, calls=%fused_computation.6 | loop fusion | bytes 2097152 | tf_op jit(solution)/shard_map/slice | solution.py:88
  421.8 6.3 fusion.17
  428.7 28.3 %all_to_all.303 = f32[16,64,256]{2,0,1:T(8,128)S(1)} all-to-all(f32[16,64,256]{2,0,1:T(8,128)S(1)} %copy.125), channel_id=1, replica_groups=mesh['bx'=16,'by'=8] {'bx'}, dimensions={1} | all-to-all | bytes 2097152 | tf_op jit(solution)/shard_map/all_to_all | solution.py:39
  460.3 19.7 %all_to_all.304 = f32[256,4,256]{2,1,0:T(4,128)S(1)} all-to-all(f32[256,4,256]{2,1,0:T(4,128)} %copy.128), channel_id=1, replica_groups=mesh['bx'=16,'by'=8] {'bx'}, dimensions={0} | all-to-all | bytes 2097152 | tf_op jit(solution)/shard_map/all_to_all | solution.py:41
  494.0 5.1 collective-permute-start.10
  503.0 19.1 %all_to_all.305 = f32[16,64,256]{2,1,0:T(8,128)S(1)} all-to-all(f32[16,64,256]{2,1,0:T(8,128)S(1)} %fusion.24), channel_id=1, replica_groups=mesh['bx'=16,'by'=8] {'by'}, dimensions={0} | all-to-all | bytes 2097152 | tf_op jit(solution)/shard_map/all_to_all | solution.py:46
  528.8 19.6 %all_to_all.306 = f32[2,512,256]{2,0,1:T(2,128)S(1)} all-to-all(f32[2,512,256]{2,0,1:T(2,128)} %copy.135), channel_id=1, replica_groups=mesh['bx'=16,'by'=8] {'by'}, dimensions={1} | all-to-all | bytes 2097152 | tf_op jit(solution)/shard_map/all_to_all | solution.py:48
  580.5 29.2 %all_to_all.307 = f32[16,64,256]{2,0,1:T(8,128)S(1)} all-to-all(f32[16,64,256]{2,0,1:T(8,128)S(1)} %copy.138), channel_id=1, replica_groups=mesh['bx'=16,'by'=8] {'bx'}, dimensions={1} | all-to-all | bytes 2097152 | tf_op jit(solution)/shard_map/all_to_all | solution.py:39
  613.0 20.0 %all_to_all.308 = f32[256,4,256]{2,1,0:T(4,128)S(1)} all-to-all(f32[256,4,256]{2,1,0:T(4,128)} %copy.141), channel_id=1, replica_groups=mesh['bx'=16,'by'=8] {'bx'}, dimensions={0} | all-to-all | bytes 2097152 | tf_op jit(solution)/shard_map/all_to_all | solution.py:41
  652.1 18.9 %all_to_all.309 = f32[16,64,256]{2,1,0:T(8,128)S(1)} all-to-all(f32[16,64,256]{2,1,0:T(8,128)S(1)} %fusion.37), channel_id=1, replica_groups=mesh['bx'=16,'by'=8] {'by'}, dimensions={0} | all-to-all | bytes 2097152 | tf_op jit(solution)/shard_map/all_to_all | solution.py:46
  677.8 19.6 %all_to_all.310 = f32[2,512,256]{2,0,1:T(2,128)S(1)} all-to-all(f32[2,512,256]{2,0,1:T(2,128)} %copy.146), channel_id=1, replica_groups=mesh['bx'=16,'by'=8] {'by'}, dimensions={1} | all-to-all | bytes 2097152 | tf_op jit(solution)/shard_map/all_to_all | solution.py:48
  729.8 26.5 %all_to_all.311 = f32[16,64,256]{2,0,1:T(8,128)S(1)} all-to-all(f32[16,64,256]{2,0,1:T(8,128)S(1)} %copy.149), channel_id=1, replica_groups=mesh['bx'=16,'by'=8] {'bx'}, dimensions={1} | all-to-all | bytes 2097152 | tf_op jit(solution)/shard_map/all_to_all | solution.py:39
  759.6 20.2 %all_to_all.312 = f32[256,4,256]{2,1,0:T(4,128)S(1)} all-to-all(f32[256,4,256]{2,1,0:T(4,128)} %copy.152), channel_id=1, replica_groups=mesh['bx'=16,'by'=8] {'bx'}, dimensions={0} | all-to-all | bytes 2097152 | tf_op jit(solution)/shard_map/all_to_all | solution.py:41
  790.3 4.8 collective-permute-start.34
  798.9 18.9 %all_to_all.313 = f32[16,64,256]{2,1,0:T(8,128)S(1)} all-to-all(f32[16,64,256]{2,1,0:T(8,128)S(1)} %fusion.50), channel_id=1, replica_groups=mesh['bx'=16,'by'=8] {'by'}, dimensions={0} | all-to-all | bytes 2097152 | tf_op jit(solution)/shard_map/all_to_all | solution.py:46
  824.6 19.6 %all_to_all.314 = f32[2,512,256]{2,0,1:T(2,128)S(1)} all-to-all(f32[2,512,256]{2,0,1:T(2,128)} %copy.157), channel_id=1, replica_groups=mesh['bx'=16,'by'=8] {'by'}, dimensions={1} | all-to-all | bytes 2097152 | tf_op jit(solution)/shard_map/all_to_all | solution.py:48
  876.6 26.8 %all_to_all.315 = f32[16,64,256]{2,0,1:T(8,128)S(1)} all-to-all(f32[16,64,256]{2,0,1:T(8,128)S(1)} %copy.160), channel_id=1, replica_groups=mesh['bx'=16,'by'=8] {'bx'}, dimensions={1} | all-to-all | bytes 2097152 | tf_op jit(solution)/shard_map/all_to_all | solution.py:39
  906.6 19.8 %all_to_all.316 = f32[256,4,256]{2,1,0:T(4,128)S(1)} all-to-all(f32[256,4,256]{2,1,0:T(4,128)} %copy.163), channel_id=1, replica_groups=mesh['bx'=16,'by'=8] {'bx'}, dimensions={0} | all-to-all | bytes 2097152 | tf_op jit(solution)/shard_map/all_to_all | solution.py:41
  937.0 4.9 collective-permute-start.46
  945.7 19.4 %all_to_all.317 = f32[16,64,256]{2,1,0:T(8,128)S(1)} all-to-all(f32[16,64,256]{2,1,0:T(8,128)S(1)} %fusion.63), channel_id=1, replica_groups=mesh['bx'=16,'by'=8] {'by'}, dimensions={0} | all-to-all | bytes 2097152 | tf_op jit(solution)/shard_map/all_to_all | solution.py:46
  971.9 19.6 %all_to_all.318 = f32[2,512,256]{2,0,1:T(2,128)S(1)} all-to-all(f32[2,512,256]{2,0,1:T(2,128)} %copy.168), channel_id=1, replica_groups=mesh['bx'=16,'by'=8] {'by'}, dimensions={1} | all-to-all | bytes 2097152 | tf_op jit(solution)/shard_map/all_to_all | solution.py:48
  1008.1 45.5 %gather_fusion = f32[8192]{0:T(1024)S(1)} fusion(f32[262144]{0:T(1024)S(1)} %bitcast.146, s32[8192]{0:T(1024)S(1)} %broadcast_clamp_fusion), kind=kCustom, calls=%fused_computation | custom fusion | bytes 98304 | tf_op jit(solution)/shard_map/gather | solution.py:105
  1054.3 10.7 all-to-all-start.18
  1065.1 9.5 all-to-all-done.18
  1076.0 40.6 %gather_fusion.1 = f32[4096]{0:T(1024)} fusion(f32[8192]{0:T(1024)S(1)} %reshape.93, s32[4096]{0:T(1024)S(1)} %broadcast_clamp_fusion.2), kind=kCustom, calls=%fused_computation.1 | custom fusion | bytes 49152 | tf_op jit(solution)/shard_map/gather | solution.py:109
  (274 shorter events, 272.2 us)
Async XLA Ops:
  24.6 30.6 %all-to-all-start = ((s32[1,128,64]{2,0,1:T(1,128)}), s32[1,128,64]{2,0,1:T(1,128)S(1)}, u32[]{:S(2)}, u32[]{:S(2)}) async-start(s32[1,128,64]{2,0,1:T(1,128)} %bitcast.7), calls=%async_computation | async-start | bytes 131072 | tf_op jit(solution)/shard_map/all_to_all | solution.py:72
  55.1 20.3 %all-to-all-start.1 = ((f32[128,1,192]{2,1,0:T(1,128)}), f32[128,1,192]{2,1,0:T(1,128)S(1)}, u32[]{:S(2)}, u32[]{:S(2)}) async-start(f32[128,1,192]{2,1,0:T(1,128)} %reshape.162), calls=%async_computation.1 | async-start | bytes 262144 | tf_op jit(solution)/shard_map/all_to_all | solution.py:65
  318.7 19.6 %collective-permute-start = (f32[3,1,64,256]{3,2,1,0:T(8,128)S(1)}, f32[3,1,64,256]{3,2,1,0:T(8,128)S(1)}, u32[]{:S(2)}, u32[]{:S(2)}) collective-permute-start(f32[3,1,64,256]{3,2,1,0:T(8,128)S(1)} %get-tuple-element.9), channel_id=1, source_target_pairs={{8,0},{16,8},{24,16},{32,24},{40,32},{48,40},{56,48},{64,56},{72,6... | collective-permute-start | bytes 589832 | tf_op jit(solution)/shard_map/ppermute | solution.py:23
  320.0 18.3 %collective-permute-start.1 = (f32[3,1,64,256]{3,2,1,0:T(8,128)S(1)}, f32[3,1,64,256]{3,2,1,0:T(8,128)S(1)}, u32[]{:S(2)}, u32[]{:S(2)}) collective-permute-start(f32[3,1,64,256]{3,2,1,0:T(8,128)S(1)} %get-tuple-element.8), channel_id=1, source_target_pairs={{0,8},{8,16},{16,24},{24,32},{32,40},{40,48},{48,56},{56,64},{64,7... | collective-permute-start | bytes 589832 | tf_op jit(solution)/shard_map/ppermute | solution.py:22
  324.0 6.1 collective-permute-start.4
  331.6 90.2 %collective-permute-start.6 = (f32[18,1,256]{2,1,0:T(1,128)}, f32[18,1,256]{2,1,0:T(1,128)}, u32[]{:S(2)}, u32[]{:S(2)}) collective-permute-start(f32[18,1,256]{2,1,0:T(1,128)} %get-tuple-element.32), channel_id=1, source_target_pairs={{1,0},{2,1},{3,2},{4,3},{5,4},{6,5},{7,6},{9,8},{10,9},{11,10},{12... | collective-permute-start | bytes 55304 | tf_op jit(solution)/shard_map/ppermute | solution.py:23
  334.9 86.8 %collective-permute-start.7 = (f32[18,1,256]{2,1,0:T(1,128)}, f32[18,1,256]{2,1,0:T(1,128)}, u32[]{:S(2)}, u32[]{:S(2)}) collective-permute-start(f32[18,1,256]{2,1,0:T(1,128)} %get-tuple-element.33), channel_id=1, source_target_pairs={{0,1},{1,2},{2,3},{3,4},{4,5},{5,6},{6,7},{8,9},{9,10},{10,11},{11... | collective-permute-start | bytes 55304 | tf_op jit(solution)/shard_map/ppermute | solution.py:22
  340.2 81.6 %collective-permute-start.2 = (f32[3,18,1,256]{3,2,1,0:T(1,128)}, f32[3,18,1,256]{3,2,1,0:T(1,128)}, u32[]{:S(2)}, u32[]{:S(2)}) collective-permute-start(f32[3,18,1,256]{3,2,1,0:T(1,128)} %get-tuple-element.6), channel_id=1, source_target_pairs={{1,0},{2,1},{3,2},{4,3},{5,4},{6,5},{7,6},{9,8},{10,9},{11,10},{12... | collective-permute-start | bytes 165896 | tf_op jit(solution)/shard_map/ppermute | solution.py:23
  342.1 79.7 %collective-permute-start.3 = (f32[3,18,1,256]{3,2,1,0:T(1,128)}, f32[3,18,1,256]{3,2,1,0:T(1,128)}, u32[]{:S(2)}, u32[]{:S(2)}) collective-permute-start(f32[3,18,1,256]{3,2,1,0:T(1,128)} %get-tuple-element.7), channel_id=1, source_target_pairs={{0,1},{1,2},{2,3},{3,4},{4,5},{5,6},{6,7},{8,9},{9,10},{10,11},{11... | collective-permute-start | bytes 165896 | tf_op jit(solution)/shard_map/ppermute | solution.py:22
  481.6 8.4 collective-permute-start.9
  494.0 7.1 collective-permute-start.10
  555.4 6.2 collective-permute-start.14
  564.1 6.3 collective-permute-start.16
  565.4 5.9 collective-permute-start.17
  571.4 6.9 collective-permute-start.18
  643.5 6.9 collective-permute-start.22
  697.7 5.9 collective-permute-start.24
  699.0 5.9 collective-permute-start.25
  713.4 6.3 collective-permute-start.28
  714.7 5.9 collective-permute-start.29
  720.7 6.9 collective-permute-start.30
  790.3 6.7 collective-permute-start.34
  844.5 5.9 collective-permute-start.36
  845.8 5.9 collective-permute-start.37
  860.2 6.3 collective-permute-start.40
  861.5 5.9 collective-permute-start.41
  867.5 6.9 collective-permute-start.42
  937.0 6.9 collective-permute-start.46
  991.9 5.9 collective-permute-start.48
  993.2 5.9 collective-permute-start.49
  999.1 5.9 collective-permute-start.50
  1054.3 20.2 %all-to-all-start.18 = ((f32[1,128,64]{2,0,1:T(1,128)}), f32[1,128,64]{2,0,1:T(1,128)S(1)}, u32[]{:S(2)}, u32[]{:S(2)}) async-start(f32[1,128,64]{2,0,1:T(1,128)} %bitcast.71), calls=%async_computation.18 | async-start | bytes 131072 | tf_op jit(solution)/shard_map/all_to_all | solution.py:106
  (42 other events, 978.3 us)
where the time goes:
time: 1130 us; the launch traced here: 1120 us
  blocking collectives  345 us (31%)
  local copies, waits for them, and re-layouts  317 us (28%)
  other arithmetic  193 us (17%)
  starting transfers between devices  188 us (17%)
  waiting for transfers between devices  40.3 us (4%)
  matrix products  30.9 us (3%)
    scatter-add x3, other arithmetic, local(): vector_field = jnp.zeros((3, brick_cells), jnp.float32).at[:, flat_cells]...  166 us
    all_to_all x4, blocking collectives, sweep_first(): lax.all_to_all(remainder, 'bx', split_axis=1, concat_axis=0, tiled=True)  111 us
    ppermute x26, starting transfers between devices, padded(): before = lax.ppermute(last, axis, up)  89.2 us
    all_to_all x4, blocking collectives, sweep_first(): lax.all_to_all(product, 'bx', split_axis=0, concat_axis=1, tiled=True)  79.6 us
    all_to_all x4, blocking collectives, sweep_second(): lax.all_to_all(product, 'by', split_axis=1, concat_axis=0, tiled=True)  78.2 us
    reshape x1, local copies, waits for them, and re-layouts, local(): vector_field = vector_field.reshape(3, CX, CY, NZ)  77.2 us
    all_to_all x4, blocking collectives, sweep_second(): lax.all_to_all(remainder, 'by', split_axis=0, concat_axis=1, tiled=True)  76.3 us
    slice x1, local copies, waits for them, and re-layouts, local(): z_padded = jnp.pad(vector_field[2], ((0, 0), (0, 0), (1, 1)))  74.8 us
  transfers between devices with their start and end apart: 55, of which 28 were waited for; matrix products, arithmetic and copies ran while one was open for 10% of the time, Pallas kernels for 0%

commit v1 on v0

--- a/solution.py
+++ b/solution.py
@@ -1,12 +1,386 @@
+import functools
 import jax
 import jax.numpy as jnp
 from jax import lax
+from jax.experimental import pallas as pl
+from jax.experimental.pallas import tpu as pltpu
 from jax.sharding import PartitionSpec as P
 
-CX = 16
-CY = 64
-NZ = 256
-ITERS = 4
+CX, CY, NZ, ITERS = 16, 64, 256, 4
+NI, NJ = 16, 8
+MESH = pl.DeviceIdType.MESH
+F32, BF16 = jnp.float32, jnp.bfloat16
+
+
+def split(v):
+    hi = v.astype(BF16)
+    return hi, (v - hi.astype(F32)).astype(BF16)
+
+
+def dot3(a_hi, a_lo, b_hi, b_lo, dims=(((1,), (0,)), ((), ()))):
+    mul = functools.partial(lax.dot_general, dimension_numbers=dims, preferred_element_type=F32)
+    return mul(a_hi, b_hi) + (mul(a_lo, b_hi) + mul(a_hi, b_lo))
+
+
+def remote(src, dst, send, recv, device):
+    return pltpu.make_async_remote_copy(
+        src_ref=src, dst_ref=dst, send_sem=send, recv_sem=recv, device_id=device, device_id_type=MESH
+    )
+
+
+def bx_peer(bx, t):
+    y, z = bx // 4, bx % 4
+    return ((y + t // 4) % 4) * 4 + (z + t % 4) % 4
+
+
+def al(v, m):
+    return pl.multiple_of(v * m, m)
+
+
+def greet(bx, by):
+    barrier = pltpu.get_barrier_semaphore()
+    count = 0
+    for side in (0, 1, NJ - 1):
+        for t in range(NI):
+            if side == 0 and t == 0:
+                continue
+            pl.semaphore_signal(
+                barrier, inc=1, device_id=(bx_peer(bx, t), (by + side) % NJ), device_id_type=MESH
+            )
+            count += 1
+    for t in range(2, NJ - 1):
+        pl.semaphore_signal(barrier, inc=1, device_id=(bx, (by + t) % NJ), device_id_type=MESH)
+        count += 1
+    pl.semaphore_wait(barrier, count)
+
+
+def relax(
+    f_ref, lev_ref, mx_ref, my_ref, mz_ref, u_ref,
+    r, xin, dxp, dx, edge, yhx, yin, dyl, dy, ye, yhy, dz, ze, yhz,
+    mxs, mys, mzs,
+    xs, xr, bs, br, es, er, ys, yr, cs, cr, ns, nr, hs, hr, zs, zr,
+):
+    bx, by = lax.axis_index("bx"), lax.axis_index("by")
+    yg, zh = bx // 2, bx % 2
+    zero = jnp.zeros((8, 128), F32)
+    dxp[0] = zero
+    dxp[257] = zero
+    for ref in (yhx, yhy, yhz):
+        ref[...] = jnp.zeros(ref.shape, F32)
+    ye[...] = jnp.zeros(ye.shape, F32)
+    for it in range(ITERS):
+        for ref in (dy, dz):
+            ref[it, 0] = jnp.zeros((CY, NZ), F32)
+            ref[it, CX + 1] = jnp.zeros((CY, NZ), F32)
+    r[...] = f_ref[...]
+    u_ref[...] = jnp.zeros(u_ref.shape, F32)
+    for m, ms in ((mx_ref, mxs), (my_ref, mys), (mz_ref, mzs)):
+        ms[0], ms[1] = split(m[...])
+    greet(bx, by)
+    diagonal = 6.0 + (1.0 + lev_ref[0, 0].astype(F32))
+
+    def stencil(d, low, high):
+        @pl.loop(0, CX)
+        def _(x):
+            c = d[x + 1]
+            zi = lax.broadcasted_iota(jnp.int32, (CY, NZ), 1)
+            yi = lax.broadcasted_iota(jnp.int32, (CY, NZ), 0)
+            near = d[x] + d[x + 2]
+            near = near + jnp.where(zi == 0, 0.0, pltpu.roll(c, 1, 1))
+            near = near + jnp.where(zi == NZ - 1, 0.0, pltpu.roll(c, NZ - 1, 1))
+            near = near + jnp.where(yi == 0, low(x), pltpu.roll(c, 1, 0))
+            near = near + jnp.where(yi == CY - 1, high(x), pltpu.roll(c, CY - 1, 0))
+            r[x] = r[x] - (diagonal * c - near)
+            u_ref[x] = u_ref[x] + c
+
+    def x_planes(d, send, recv):
+        down = remote(d.at[1], d.at[CX + 1], send.at[0], recv.at[0], (jnp.maximum(bx - 1, 0), by))
+        up = remote(d.at[CX], d.at[0], send.at[1], recv.at[1], (jnp.minimum(bx + 1, NI - 1), by))
+        return down, up
+
+    @pl.loop(0, ITERS)
+    def _(it):
+        copies = []
+        for t in range(NI):
+            k = bx_peer(bx, t)
+            src = r.at[:, pl.ds(al(k // 2, 8), 8), pl.ds(al(k % 2, 128), 128)]
+            dst = xin.at[it, pl.ds(bx * 16, 16)]
+            if t:
+                copies.append(remote(src, dst, xs.at[t], xr.at[t], (k, by)))
+            else:
+                copies.append(pltpu.make_async_copy(src, dst, xs.at[0]))
+            copies[-1].start()
+        for c in copies:
+            c.wait()
+        lines = xin.at[it].reshape(NI * CX * 8, 128)
+        moved = dxp.reshape((NI * CX + 2) * 8, 128)
+        for s in range(0, 8, 2):
+            v = jnp.concatenate(
+                [lines[pl.ds(s, 256, stride=8), :], lines[pl.ds(s + 1, 256, stride=8), :]], axis=1
+            )
+            d = dot3(mxs[0], mxs[1], *split(v))
+            moved[pl.ds(8 + s, 256, stride=8), :] = d[:, :128]
+            moved[pl.ds(9 + s, 256, stride=8), :] = d[:, 128:]
+            if s == 0:
+                edge[0] = d[:, :128]
+            if s == 6:
+                edge[1] = d[:, 128:]
+        copies = []
+        for t in range(NI):
+            k = bx_peer(bx, t)
+            src = dxp.at[pl.ds(k * 16, 18)]
+            dst = dx.at[it, :, pl.ds(al(yg, 8), 8), pl.ds(al(zh, 128), 128)]
+            if t:
+                copies.append(remote(src, dst, bs.at[t], br.at[t], (k, by)))
+            else:
+                copies.append(pltpu.make_async_copy(src, dst, bs.at[0]))
+            copies[-1].start()
+
+        def edges(side, beside):
+            out = []
+            for t in range(NI):
+                k = bx_peer(bx, t)
+                out.append(
+                    remote(
+                        edge.at[side, pl.ds(al(k, 16), 16)],
+                        yhx.at[it, side, :, pl.ds(al(zh, 128), 128)],
+                        es.at[side, t],
+                        er.at[side, zh],
+                        (k, beside),
+                    )
+                )
+            return out
+
+        def half(side, z):
+            return remote(
+                edge.at[side, pl.ds(0, 16)], yhx.at[it, side, :, pl.ds(128 * z, 128)],
+                es.at[side, 0], er.at[side, z], (bx, by),
+            )
+
+        below, above = jnp.maximum(by - 1, 0), jnp.minimum(by + 1, NJ - 1)
+
+        @pl.when((yg == 0) & (by > 0))
+        def _():
+            for c in edges(0, below):
+                c.start()
+
+        @pl.when((yg == 7) & (by < NJ - 1))
+        def _():
+            for c in edges(1, above):
+                c.start()
+
+        for c in copies:
+            c.wait()
+
+        @pl.when((yg == 0) & (by > 0))
+        def _():
+            for c in edges(0, below):
+                c.wait_send()
+
+        @pl.when((yg == 7) & (by < NJ - 1))
+        def _():
+            for c in edges(1, above):
+                c.wait_send()
+
+        @pl.when(by < NJ - 1)
+        def _():
+            half(0, 0).wait_recv()
+            half(0, 1).wait_recv()
+
+        @pl.when(by > 0)
+        def _():
+            half(1, 0).wait_recv()
+            half(1, 1).wait_recv()
+
+        stencil(
+            dx.at[it],
+            lambda x: yhx[it, 1, pl.ds(x, 1), :],
+            lambda x: yhx[it, 0, pl.ds(x, 1), :],
+        )
+
+        copies = []
+        for t in range(NJ):
+            j = (by + t) % NJ
+            src = r.at[pl.ds(2 * j, 2)]
+            dst = yin.at[it, :, pl.ds(al(by, 64), 64), :]
+            if t:
+                copies.append(remote(src, dst, ys.at[t], yr.at[t], (bx, j)))
+            else:
+                copies.append(pltpu.make_async_copy(src, dst, ys.at[0]))
+            copies[-1].start()
+        for c in copies:
+            c.wait()
+        for e in range(2):
+            d = dot3(mys[0], mys[1], *split(yin[it, e]))
+            dyl[e] = d
+            for j in range(NJ):
+                if j:
+                    ye[j, e : e + 1] = d[64 * j - 1 : 64 * j]
+                if j < NJ - 1:
+                    ye[j, 2 + e : 3 + e] = d[64 * j + 64 : 64 * j + 65]
+        copies = []
+        for t in range(NJ):
+            j = (by + t) % NJ
+            main = (dyl.at[:, pl.ds(al(j, 64), 64), :], dy.at[it, pl.ds(1 + 2 * by, 2)])
+            rows = (ye.at[j], yhy.at[it, by])
+            if t:
+                copies.append(remote(*main, cs.at[t], cr.at[by], (bx, j)))
+                copies.append(remote(*rows, ns.at[t], nr.at[t], (bx, j)))
+            else:
+                copies.append(pltpu.make_async_copy(*main, cr.at[by]))
+                copies.append(pltpu.make_async_copy(*rows, ns.at[0]))
+            copies[-2].start()
+            copies[-1].start()
+
+        def arrived(m):
+            remote(
+                dyl.at[:, pl.ds(0, 64), :], dy.at[it, pl.ds(1 + 2 * m, 2)], cs.at[0], cr.at[m], (bx, by)
+            ).wait_recv()
+
+        down, up = x_planes(dy.at[it], hs, hr)
+        arrived(0)
+
+        @pl.when(bx > 0)
+        def _():
+            down.start()
+
+        arrived(NJ - 1)
+
+        @pl.when(bx < NI - 1)
+        def _():
+            up.start()
+
+        for m in range(1, NJ - 1):
+            arrived(m)
+        for t in range(1, NJ):
+            copies[2 * t].wait_send()
+            copies[2 * t + 1].wait()
+        copies[1].wait()
+
+        @pl.when(bx > 0)
+        def _():
+            down.wait_send()
+            up.wait_recv()
+
+        @pl.when(bx < NI - 1)
+        def _():
+            up.wait_send()
+            down.wait_recv()
+
+        stencil(
+            dy.at[it],
+            lambda x: yhy[it, x // 2, pl.ds(x % 2, 1), :],
+            lambda x: yhy[it, x // 2, pl.ds(2 + x % 2, 1), :],
+        )
+
+        nt = (((1,), (1,)), ((), ()))
+
+        def z_planes(x, n):
+            v = r[pl.ds(x, n)].reshape(n * CY, NZ)
+            d = dot3(*split(v), mzs[0], mzs[1], nt)
+            dz[it, pl.ds(x + 1, n)] = d.reshape(n, CY, NZ)
+
+        z_planes(0, 1)
+        z_planes(CX - 1, 1)
+        down, up = x_planes(dz.at[it], zs, zr)
+        more = it < ITERS - 1
+
+        @pl.when(more & (bx > 0))
+        def _():
+            down.start()
+
+        @pl.when(more & (bx < NI - 1))
+        def _():
+            up.start()
+
+        for x in range(1, CX - 1, 2):
+            z_planes(x, 2)
+
+        @pl.when(more)
+        def _():
+            for x in range(CX):
+                ze[0, x : x + 1] = dz[it, x + 1, 0:1]
+                ze[1, x : x + 1] = dz[it, x + 1, CY - 1 : CY]
+            low = remote(ze.at[0], yhz.at[it, 0], zs.at[2], zr.at[2], (bx, below))
+            high = remote(ze.at[1], yhz.at[it, 1], zs.at[3], zr.at[3], (bx, above))
+
+            @pl.when(by > 0)
+            def _():
+                low.start()
+
+            @pl.when(by < NJ - 1)
+            def _():
+                high.start()
+
+            @pl.when(by > 0)
+            def _():
+                low.wait_send()
+                high.wait_recv()
+
+            @pl.when(by < NJ - 1)
+            def _():
+                high.wait_send()
+                low.wait_recv()
+
+            @pl.when(bx > 0)
+            def _():
+                down.wait_send()
+                up.wait_recv()
+
+            @pl.when(bx < NI - 1)
+            def _():
+                up.wait_send()
+                down.wait_recv()
+
+            stencil(
+                dz.at[it],
+                lambda x: yhz[it, 1, pl.ds(x, 1), :],
+                lambda x: yhz[it, 0, pl.ds(x, 1), :],
+            )
+
+        @pl.when(it == ITERS - 1)
+        def _():
+            u_ref[...] = u_ref[...] + dz[it, pl.ds(1, CX)]
+
+
+def relaxed(source, levels, rows, columns, depth):
+    vm = pl.BlockSpec(memory_space=pltpu.VMEM)
+    brick = (CX, CY, NZ)
+    tall = (ITERS, CX + 2, CY, NZ)
+    dma = pltpu.SemaphoreType.DMA
+    return pl.pallas_call(
+        relax,
+        name="relax",
+        out_shape=jax.ShapeDtypeStruct(brick, F32),
+        in_specs=[vm, pl.BlockSpec(memory_space=pltpu.SMEM), vm, vm, vm],
+        out_specs=vm,
+        scratch_shapes=[
+            pltpu.VMEM(brick, F32),
+            pltpu.VMEM((ITERS, NI * CX, 8, 128), F32),
+            pltpu.VMEM((NI * CX + 2, 8, 128), F32),
+            pltpu.VMEM(tall, F32),
+            pltpu.VMEM((2, NI * CX, 128), F32),
+            pltpu.VMEM((ITERS, 2, CX, NZ), F32),
+            pltpu.VMEM((ITERS, 2, NJ * CY, NZ), F32),
+            pltpu.VMEM((2, NJ * CY, NZ), F32),
+            pltpu.VMEM(tall, F32),
+            pltpu.VMEM((NJ, 8, NZ), F32),
+            pltpu.VMEM((ITERS, NJ, 8, NZ), F32),
+            pltpu.VMEM(tall, F32),
+            pltpu.VMEM((2, CX, NZ), F32),
+            pltpu.VMEM((ITERS, 2, CX, NZ), F32),
+            pltpu.VMEM((2, 256, 256), BF16),
+            pltpu.VMEM((2, 512, 512), BF16),
+            pltpu.VMEM((2, 256, 256), BF16),
+            dma((NI,)), dma((NI,)), dma((NI,)), dma((NI,)),
+            dma((2, NI)), dma((2, 2)),
+            dma((NJ,)), dma((NJ,)), dma((NJ,)), dma((NJ,)), dma((NJ,)), dma((NJ,)),
+            dma((2,)), dma((2,)), dma((4,)), dma((4,)),
+        ],
+        compiler_params=pltpu.CompilerParams(
+            collective_id=0, has_side_effects=True, vmem_limit_bytes=52 << 20
+        ),
+    )(source, levels, rows, columns, depth)
 
 
 screen_base = 1.0
@@ -23,29 +397,6 @@
         after = lax.ppermute(initial, axis, down)
         shard = jnp.concatenate([before, shard, after], axis=dim)
     return shard
-
-
-def remainder_of(iterate, source, screening):
-    extended = padded(iterate, (("bx", 0), ("by", 1)), 1)
-    z_padded = jnp.pad(iterate, ((0, 0), (0, 0), (1, 1)))
-    beside = extended[2:, 1:-1] + extended[:-2, 1:-1]
-    beside = beside + extended[1:-1, 2:] + extended[1:-1, :-2]
-    beside = beside + z_padded[:, :, 2:] + z_padded[:, :, :-2]
-    return source - ((6.0 + screening) * iterate - beside)
-
-
-def sweep_first(remainder, matrix):
-    highest = lax.Precision.HIGHEST
-    lines = lax.all_to_all(remainder, "bx", split_axis=1, concat_axis=0, tiled=True)
-    product = jnp.einsum("ab,bjk->ajk", matrix, lines, precision=highest)
-    return lax.all_to_all(product, "bx", split_axis=0, concat_axis=1, tiled=True)
-
-
-def sweep_second(remainder, matrix):
-    highest = lax.Precision.HIGHEST
-    lines = lax.all_to_all(remainder, "by", split_axis=0, concat_axis=1, tiled=True)
-    product = jnp.einsum("ab,ibk->iak", matrix, lines, precision=highest)
-    return lax.all_to_all(product, "by", split_axis=1, concat_axis=0, tiled=True)
 
 
 def local(normals, owners, cells, levels, rows_inverse, columns_inverse, depth_inverse):
@@ -92,16 +443,7 @@
         + (stretched[1, 1:-1, 2:] - stretched[1, 1:-1, :-2])
         + (z_padded[:, :, 2:] - z_padded[:, :, :-2])
     )
-    screening = screen_base * (1.0 + levels[0, 0].astype(jnp.float32))
-    highest = lax.Precision.HIGHEST
-    iterate = jnp.zeros((CX, CY, NZ), jnp.float32)
-    for iteration in range(ITERS):
-        remainder = remainder_of(iterate, source, screening)
-        iterate = iterate + sweep_first(remainder, rows_inverse)
-        remainder = remainder_of(iterate, source, screening)
-        iterate = iterate + sweep_second(remainder, columns_inverse)
-        remainder = remainder_of(iterate, source, screening)
-        iterate = iterate + jnp.einsum("ab,ijb->ija", depth_inverse, remainder, precision=highest)
+    iterate = relaxed(source, levels, rows_inverse, columns_inverse, depth_inverse)
     sampled = iterate.reshape(-1)[flat_cells]
     returned = lax.all_to_all(
         sampled.reshape(1, bricks, capacity), ("bx", "by"), split_axis=1, concat_axis=1, tiled=True

time: 1130 us -> 831 us (0.74)
  blocking collectives: 345 us -> 0 us
  Pallas kernels: 0 us -> 304 us
  starting transfers between devices: 188 us -> 44.9 us
  local copies, waits for them, and re-layouts: 317 us -> 283 us
  matrix products: 30.9 us -> 0 us
  waiting for transfers between devices: 40.3 us -> 13.6 us
  other arithmetic: 193 us -> 176 us
    all_to_all x16 -> x0, blocking collectives: 345 us -> none  [the longest x4 111 us: sweep_first(): lax.all_to_all(remainder, 'bx', split_axis=1, concat_axis=0, tiled=True)]
    pallas_call x0 -> x1, Pallas kernels: none -> 304 us  [relaxed(): pl.pallas_call(relax, name='relax', out_shape=jax.ShapeDtypeStruct(brick,...]
    ppermute x26 -> x2, starting transfers between devices: 89.2 us -> 9.31 us  [padded(): before = lax.ppermute(last, axis, up)]
    ppermute x26 -> x2, starting transfers between devices: 66 us -> 3.21 us  [padded(): after = lax.ppermute(initial, axis, down)]
    dot_general x12 -> x0, matrix products: 30.9 us -> none  [the longest x4 17.8 us: sweep_second(): product = jnp.einsum('ab,ibk->iak', matrix, lines, precision=highest)]
    ppermute x26 -> x2, waiting for transfers between devices: 23.4 us -> 0.88 us  [padded(): before = lax.ppermute(last, axis, up)]
    all_to_all x28 -> x0, local copies, waits for them, and re-layouts: 11.6 us -> none  [the longest x12 10.2 us: sweep_first(): lax.all_to_all(product, 'bx', split_axis=0, concat_axis=1, tiled=True)]
    sub x8 -> x0, other arithmetic: 11.3 us -> none  [remainder_of(): return source - ((6.0 + screening) * iterate - beside)]
  transfers between devices with their start and end apart: 55 -> 7, of which waited for: 28 -> 4; matrix products, arithmetic and copies ran while one was open for 10% -> 13% of each run, Pallas kernels for 0% -> 0%
where the time goes in v1:
time: 831 us; the launch traced here: 823 us
  Pallas kernels  304 us (37%)
  local copies, waits for them, and re-layouts  283 us (34%)
  other arithmetic  176 us (21%)
  starting transfers between devices  44.9 us (5%)
  waiting for transfers between devices  13.6 us (2%)
    pallas_call x1, Pallas kernels, relaxed(): pl.pallas_call(relax, name='relax', out_shape=jax.ShapeDtypeStruct(brick,...  304 us
    scatter-add x3, other arithmetic, local(): vector_field = jnp.zeros((3, brick_cells), jnp.float32).at[:, flat_cells]...  166 us
    reshape x1, local copies, waits for them, and re-layouts, local(): vector_field = vector_field.reshape(3, CX, CY, NZ)  76 us
    slice x1, local copies, waits for them, and re-layouts, local(): z_padded = jnp.pad(vector_field[2], ((0, 0), (0, 0), (1, 1)))  75.7 us
    gather x1, local copies, waits for them, and re-layouts, local(): sampled = iterate.reshape(-1)[flat_cells]  45.5 us
    gather x1, local copies, waits for them, and re-layouts, local(): implicit = returned.reshape(-1)[slot_index]  40.6 us
  transfers between devices with their start and end apart: 7, of which 4 were waited for; matrix products, arithmetic and copies ran while one was open for 13% of the time, Pallas kernels for 0%

profile of v1, /device:TPU:1, one launch (start us, length us, event | category | flops | bytes accessed | tf_op | source)
XLA Modules:
  0.0 823.0 jit_solution(3453732715782024831)
XLA Ops:
  0.6 0.8 copy.23
  2.4 1.2 copy.24
  3.7 1.4 fusion.6
  5.1 15.7 %scatter_custom_fusion = s32[8192]{0:T(1024)S(1)} fusion(s32[4096]{0:T(1024)S(1)} %bitcast.41, s32[4096]{0:T(1024)} %param.9, s32[]{:T(128)} %constant.8.clone.1), kind=kCustom, calls=%fused_computation.45 | custom fusion | bytes 33280 | tf_op jit(solution)/shard_map/scatter | solution.py:414
  21.6 11.5 %all-to-all-start = ((s32[1,128,64]{2,0,1:T(1,128)}), s32[1,128,64]{2,0,1:T(1,128)S(1)}, u32[]{:S(2)}, u32[]{:S(2)}) async-start(s32[1,128,64]{2,0,1:T(1,128)} %bitcast.7), calls=%async_computation | async-start | bytes 131072 | tf_op jit(solution)/shard_map/all_to_all | solution.py:423
  33.7 12.8 %scatter_custom_fusion.1 = f32[3,8192]{0,1:T(8,128)} fusion(s32[4096]{0:T(1024)S(1)} %bitcast.42, f32[4096,3]{1,0:T(8,128)S(1)} %copy.26, f32[]{:T(128)} %constant.7.clone.1), kind=kCustom, calls=%fused_computation.12 | custom fusion | bytes 98308 | tf_op jit(solution)/shard_map/scatter | solution.py:413
  46.5 3.0 copy.27
  49.5 0.9 reshape.154
  51.0 10.3 %all-to-all-start.1 = ((f32[128,1,192]{2,1,0:T(1,128)}), f32[128,1,192]{2,1,0:T(1,128)S(1)}, u32[]{:S(2)}, u32[]{:S(2)}) async-start(f32[128,1,192]{2,1,0:T(1,128)} %reshape.154), calls=%async_computation.1 | async-start | bytes 262144 | tf_op jit(solution)/shard_map/all_to_all | solution.py:416
  61.9 0.8 reduce.8
  62.9 5.9 sort
  68.8 2.5 all-to-all-done.1
  71.9 1.0 reduce.10
  73.1 2.6 copy.29
  75.8 160.0 %scatter_custom_fusion.2 = f32[3,262144]{0,1:T(8,128)} fusion(s32[8192]{0:T(1024)S(1)} %get-tuple-element.2, f32[]{:T(128)} %constant.7.clone.1, f32[8192,3]{1,0:T(8,128)} %copy.29, s32[8192]{0:T(1024)S(1)} %broadcast_clamp_fusion.1), kind=kCustom, calls=%fused_computation.7 | custom fusion | flops 24576 | bytes 3146240 | tf_op jit(solution)/shard_map/scatter-add | solution.py:435
  235.8 76.0 %copy.32 = f32[3,16,64,256]{3,2,1,0:T(8,128)S(1)} copy(f32[3,16,64,256]{0,3,2,1:T(8,128)} %bitcast.12) | data formatting | bytes 6291456 | tf_op jit(solution)/shard_map/reshape | solution.py:437
  311.8 1.3 collective-permute-start
  313.1 4.0 collective-permute-start.1
  317.1 1.4 broadcast_clamp_fusion
  319.3 0.9 collective-permute-done.1
  320.9 5.3 collective-permute-start.3
  326.2 1.9 collective-permute-start.2
  328.1 75.7 %slice_reduce_fusion = f32[262144]{0:T(1024)} fusion(f32[3,262144]{0,1:T(8,128)} %scatter_custom_fusion.2), kind=kLoop, calls=%fused_computation.6 | loop fusion | bytes 2097152 | tf_op jit(solution)/shard_map/slice | solution.py:439
  403.8 2.5 squeeze.2
  406.4 3.2 fusion.13.f_ref
  409.6 303.5 %relax.1 = f32[16,64,256]{2,1,0:T(8,128)S(1)} custom-call(f32[16,64,256]{2,1,0:T(8,128)} %fusion.13.f_ref, s32[1,1]{1,0:T(1,128)S(6)} %copy.35.lev_ref, f32[256,256]{1,0:T(8,128)S(1)} %copy-done, f32[512,512]{1,0:T(8,128)} %my_ref.1, f32[256,256]{1,0:T(8,128)S(1)} %copy-done.1), custom_call_target="tpu_custom_call" | custom-call | tf_op jit(solution)/shard_map/relax/pallas_call | solution.py:351
  713.7 45.5 %gather_fusion = f32[8192]{0:T(1024)S(1)} fusion(f32[262144]{0:T(1024)S(1)} %bitcast.30, s32[8192]{0:T(1024)S(1)} %copy-done.4), kind=kCustom, calls=%fused_computation | custom fusion | bytes 98304 | tf_op jit(solution)/shard_map/gather | solution.py:447
  759.9 10.5 %all-to-all-start.2 = ((f32[1,128,64]{2,0,1:T(1,128)}), f32[1,128,64]{2,0,1:T(1,128)S(1)}, u32[]{:S(2)}, u32[]{:S(2)}) async-start(f32[1,128,64]{2,0,1:T(1,128)} %bitcast.14), calls=%async_computation.2 | async-start | bytes 131072 | tf_op jit(solution)/shard_map/all_to_all | solution.py:448
  770.5 9.4 %all-to-all-done.2 = f32[1,128,64]{2,0,1:T(1,128)S(1)} async-done(((f32[1,128,64]{2,0,1:T(1,128)}), f32[1,128,64]{2,0,1:T(1,128)S(1)}, u32[]{:S(2)}, u32[]{:S(2)}) %all-to-all-start.2) | async-done | bytes 32800 | tf_op jit(solution)/shard_map/all_to_all | solution.py:448
  780.4 0.8 reduce.9
  781.3 40.6 %gather_fusion.1 = f32[4096]{0:T(1024)} fusion(f32[8192]{0:T(1024)S(1)} %reshape.88, s32[4096]{0:T(1024)S(1)} %broadcast_clamp_fusion.2), kind=kCustom, calls=%fused_computation.1 | custom fusion | bytes 49152 | tf_op jit(solution)/shard_map/gather | solution.py:451
  821.8 1.0 copy.36
  (40 shorter events, 7.1 us)
Async XLA Ops:
  2.4 1.3 copy-start.3
  2.4 30.7 %copy-start.5 = (f32[3,4096]{1,0:T(4,128)S(1)}, f32[3,4096]{1,0:T(4,128)}, u32[]{:S(2)}) copy-start(f32[3,4096]{1,0:T(4,128)} %param.7) | copy-start | bytes 147460
  21.6 29.5 %all-to-all-start = ((s32[1,128,64]{2,0,1:T(1,128)}), s32[1,128,64]{2,0,1:T(1,128)S(1)}, u32[]{:S(2)}, u32[]{:S(2)}) async-start(s32[1,128,64]{2,0,1:T(1,128)} %bitcast.7), calls=%async_computation | async-start | bytes 131072 | tf_op jit(solution)/shard_map/all_to_all | solution.py:423
  51.0 20.3 %all-to-all-start.1 = ((f32[128,1,192]{2,1,0:T(1,128)}), f32[128,1,192]{2,1,0:T(1,128)S(1)}, u32[]{:S(2)}, u32[]{:S(2)}) async-start(f32[128,1,192]{2,1,0:T(1,128)} %reshape.154), calls=%async_computation.1 | async-start | bytes 262144 | tf_op jit(solution)/shard_map/all_to_all | solution.py:416
  62.9 9.0 %copy-start.2 = (s32[8192,1]{0,1:T(1,128)}, s32[8192,1]{0,1:T(1,128)S(1)}, u32[]{:S(2)}) copy-start(s32[8192,1]{0,1:T(1,128)S(1)} %compare_select_fusion) | copy-start | bytes 98308
  311.8 7.4 collective-permute-start
  313.1 7.0 collective-permute-start.1
  320.9 85.5 %collective-permute-start.3 = (f32[3,18,1,256]{3,2,1,0:T(1,128)}, f32[3,18,1,256]{3,2,1,0:T(1,128)}, u32[]{:S(2)}, u32[]{:S(2)}) collective-permute-start(f32[3,18,1,256]{3,2,1,0:T(1,128)} %get-tuple-element.5), channel_id=1, source_target_pairs={{0,1},{1,2},{2,3},{3,4},{4,5},{5,6},{6,7},{8,9},{9,10},{10,11},{11... | collective-permute-start | bytes 165896 | tf_op jit(solution)/shard_map/ppermute | solution.py:396
  326.2 80.2 %collective-permute-start.2 = (f32[3,18,1,256]{3,2,1,0:T(1,128)}, f32[3,18,1,256]{3,2,1,0:T(1,128)}, u32[]{:S(2)}, u32[]{:S(2)}) collective-permute-start(f32[3,18,1,256]{3,2,1,0:T(1,128)} %get-tuple-element.4), channel_id=1, source_target_pairs={{1,0},{2,1},{3,2},{4,3},{5,4},{6,5},{7,6},{9,8},{10,9},{11,10},{12... | collective-permute-start | bytes 165896 | tf_op jit(solution)/shard_map/ppermute | solution.py:397
  406.3 3.2 copy-start
  406.3 3.2 copy-start.1
  409.5 304.1 %copy-start.4 = (s32[8192]{0:T(1024)S(1)}, s32[8192]{0:T(1024)}, u32[]{:S(2)}) copy-start(s32[8192]{0:T(1024)} %broadcast_clamp_fusion) | copy-start | bytes 98308
  759.9 20.0 %all-to-all-start.2 = ((f32[1,128,64]{2,0,1:T(1,128)}), f32[1,128,64]{2,0,1:T(1,128)S(1)}, u32[]{:S(2)}, u32[]{:S(2)}) async-start(f32[1,128,64]{2,0,1:T(1,128)} %bitcast.14), calls=%async_computation.2 | async-start | bytes 131072 | tf_op jit(solution)/shard_map/all_to_all | solution.py:448

commit v2 on v1

--- a/solution.py
+++ b/solution.py
@@ -8,6 +8,7 @@
 
 CX, CY, NZ, ITERS = 16, 64, 256, 4
 NI, NJ = 16, 8
+NB, P_DEV, CAP = 128, 4096, 64
 MESH = pl.DeviceIdType.MESH
 F32, BF16 = jnp.float32, jnp.bfloat16
 
@@ -55,10 +56,12 @@
 
 
 def relax(
-    f_ref, lev_ref, mx_ref, my_ref, mz_ref, u_ref,
+    nrm, own, cel, lev_ref, mx_ref, my_ref, mz_ref, u_ref, imp_ref,
     r, xin, dxp, dx, edge, yhx, yin, dyl, dy, ye, yhy, dz, ze, yhz,
     mxs, mys, mzs,
+    box, rank, in1, out2, in2, slot, part, vx, vy, vz, fe, fh, smp, ut, back1, got1, back2, got2,
     xs, xr, bs, br, es, er, ys, yr, cs, cr, ns, nr, hs, hr, zs, zr,
+    ps, pr, qs, qr, fs, fr, gs, gr, ks, kr,
 ):
     bx, by = lax.axis_index("bx"), lax.axis_index("by")
     yg, zh = bx // 2, bx % 2
@@ -72,11 +75,169 @@
         for ref in (dy, dz):
             ref[it, 0] = jnp.zeros((CY, NZ), F32)
             ref[it, CX + 1] = jnp.zeros((CY, NZ), F32)
-    r[...] = f_ref[...]
+    vx[0] = jnp.zeros((CY, NZ), F32)
+    vx[CX + 1] = jnp.zeros((CY, NZ), F32)
+    vx[pl.ds(1, CX)] = jnp.zeros((CX, CY, NZ), F32)
+    vy[...] = jnp.zeros(vy.shape, F32)
+    vz[...] = jnp.zeros(vz.shape, F32)
+    fh[...] = jnp.zeros(fh.shape, F32)
     u_ref[...] = jnp.zeros(u_ref.shape, F32)
     for m, ms in ((mx_ref, mxs), (my_ref, mys), (mz_ref, mzs)):
         ms[0], ms[1] = split(m[...])
     greet(bx, by)
+    below, above = jnp.maximum(by - 1, 0), jnp.minimum(by + 1, NJ - 1)
+    lanes = (((1,), (1,)), ((), ()))
+
+    def fit(rows, index):
+        return lax.broadcasted_iota(jnp.int32, (rows, index.shape[1]), 0) == index
+
+    def hot(mask):
+        return jnp.where(mask, 1.0, 0.0).astype(BF16)
+
+    def chop(v, n):
+        pieces = []
+        for _ in range(n):
+            pieces.append(v.astype(BF16).astype(F32))
+            v = v - pieces[-1]
+        return pieces
+
+    before = lax.broadcasted_iota(jnp.int32, (256, 256), 0) < lax.broadcasted_iota(jnp.int32, (256, 256), 1)
+    counter = jnp.concatenate([hot(before), jnp.ones((256, 256), BF16)], axis=1)
+    box[...] = jnp.zeros(box.shape, F32)
+
+    def dispatch(c, seen):
+        at = pl.ds(al(c, 256), 256)
+        mine = fit(NB, own[:, at])
+        ones = hot(mine)
+        counts = jnp.dot(ones, counter, preferred_element_type=F32)
+        place = jnp.sum(jnp.where(mine, counts[:, :256] + seen, 0.0), axis=0, keepdims=True)
+        place = place.astype(jnp.int32)
+        rank[:, at] = place
+        there = fit(CAP, place)
+        values = [nrm[k : k + 1, at] for k in range(3)] + [cel[:, at].astype(F32)]
+        pieces = [chop(v, 3) for v in values]
+        for n in range(3):
+            w = jnp.concatenate([jnp.where(there, p[n], 0.0) for p in pieces], axis=0).astype(BF16)
+            d = lax.dot_general(ones, w, lanes, preferred_element_type=F32)
+            box[0] += d[:, :128]
+            box[1] += d[:, 128:]
+        return seen + counts[:, 256:]
+
+    lax.fori_loop(0, P_DEV // 256, dispatch, jnp.zeros((NB, 256), F32))
+
+    copies = []
+    for t in range(NI):
+        k = bx_peer(bx, t)
+        src, dst = box.at[:, pl.ds(al(k, 8), 8)], in1.at[:, pl.ds(al(bx, 8), 8)]
+        if t:
+            copies.append(remote(src, dst, ps.at[t], pr.at[t], (k, by)))
+        else:
+            copies.append(pltpu.make_async_copy(src, dst, ps.at[0]))
+        copies[-1].start()
+    for c in copies:
+        c.wait()
+    for j in range(NJ):
+        for h in range(2):
+            out2[j, h] = in1.at[h][pl.ds(j, NI, stride=NJ), :]
+    copies = []
+    for t in range(NJ):
+        j = (by + t) % NJ
+        if t:
+            copies.append(remote(out2.at[j], in2.at[by], qs.at[t], qr.at[t], (bx, j)))
+        else:
+            copies.append(pltpu.make_async_copy(out2.at[j], in2.at[by], qs.at[0]))
+        copies[-1].start()
+    for c in copies:
+        c.wait()
+
+    for k in range(4):
+        v = in2[:, k // 2].reshape(NB, 128)[:, CAP * (k % 2) : CAP * (k % 2 + 1)]
+        v = jnp.concatenate([v[: NB // 2], v[NB // 2 :]], axis=1)
+        v = jnp.concatenate([v[: NB // 4], v[NB // 4 :]], axis=1)
+        if k < 3:
+            part[2 * k], part[2 * k + 1] = chop(v, 2)
+        else:
+            slot[...] = v.astype(jnp.int32)
+
+    @pl.loop(0, NB // 4)
+    def _(c):
+        cell = slot[pl.ds(c, 1), :]
+        depth = fit(NZ, cell % NZ)
+        weighted = jnp.concatenate(
+            [
+                jnp.concatenate(
+                    [jnp.where(depth, part[2 * k + n, pl.ds(c, 1), :], 0.0).astype(BF16) for n in range(2)],
+                    axis=1,
+                )
+                for k in range(3)
+            ],
+            axis=0,
+        )
+        for q in range(4):
+            a = hot(fit(256, cell // NZ - 256 * q))
+            d = lax.dot_general(
+                jnp.concatenate([a, a], axis=1), weighted, lanes, preferred_element_type=F32
+            ).reshape(4, CY, 3 * NZ)
+            vx[pl.ds(1 + 4 * q, 4)] += d[:, :, :NZ]
+            vy[pl.ds(4 * q, 4)] += d[:, :, NZ : 2 * NZ]
+            vz[pl.ds(4 * q, 4)] += d[:, :, 2 * NZ :]
+
+    down = remote(vx.at[1], vx.at[CX + 1], fs.at[0], fr.at[0], (jnp.maximum(bx - 1, 0), by))
+    up = remote(vx.at[CX], vx.at[0], fs.at[1], fr.at[1], (jnp.minimum(bx + 1, NI - 1), by))
+    for x in range(CX):
+        fe[0, x : x + 1] = vy[x, 0:1]
+        fe[1, x : x + 1] = vy[x, CY - 1 : CY]
+    low = remote(fe.at[0], fh.at[0], fs.at[2], fr.at[2], (bx, below))
+    high = remote(fe.at[1], fh.at[1], fs.at[3], fr.at[3], (bx, above))
+
+    @pl.when(bx > 0)
+    def _():
+        down.start()
+
+    @pl.when(bx < NI - 1)
+    def _():
+        up.start()
+
+    @pl.when(by > 0)
+    def _():
+        low.start()
+
+    @pl.when(by < NJ - 1)
+    def _():
+        high.start()
+
+    @pl.when(by > 0)
+    def _():
+        low.wait_send()
+        high.wait_recv()
+
+    @pl.when(by < NJ - 1)
+    def _():
+        high.wait_send()
+        low.wait_recv()
+
+    @pl.when(bx > 0)
+    def _():
+        down.wait_send()
+        up.wait_recv()
+
+    @pl.when(bx < NI - 1)
+    def _():
+        up.wait_send()
+        down.wait_recv()
+
+    @pl.loop(0, CX)
+    def _(x):
+        zi = lax.broadcasted_iota(jnp.int32, (CY, NZ), 1)
+        yi = lax.broadcasted_iota(jnp.int32, (CY, NZ), 0)
+        b, c = vy[x], vz[x]
+        total = vx[x + 2] - vx[x]
+        total = total + jnp.where(yi == CY - 1, fh[0, pl.ds(x, 1), :], pltpu.roll(b, CY - 1, 0))
+        total = total - jnp.where(yi == 0, fh[1, pl.ds(x, 1), :], pltpu.roll(b, 1, 0))
+        total = total + jnp.where(zi == NZ - 1, 0.0, pltpu.roll(c, NZ - 1, 1))
+        total = total - jnp.where(zi == 0, 0.0, pltpu.roll(c, 1, 1))
+        r[x] = -0.5 * total
+
     diagonal = 6.0 + (1.0 + lev_ref[0, 0].astype(F32))
 
     def stencil(d, low, high):
@@ -157,8 +318,6 @@
                 es.at[side, 0], er.at[side, z], (bx, by),
             )
 
-        below, above = jnp.maximum(by - 1, 0), jnp.minimum(by + 1, NJ - 1)
-
         @pl.when((yg == 0) & (by > 0))
         def _():
             for c in edges(0, below):
@@ -273,11 +432,10 @@
             lambda x: yhy[it, x // 2, pl.ds(2 + x % 2, 1), :],
         )
 
-        nt = (((1,), (1,)), ((), ()))
 
         def z_planes(x, n):
             v = r[pl.ds(x, n)].reshape(n * CY, NZ)
-            d = dot3(*split(v), mzs[0], mzs[1], nt)
+            d = dot3(*split(v), mzs[0], mzs[1], lanes)
             dz[it, pl.ds(x + 1, n)] = d.reshape(n, CY, NZ)
 
         z_planes(0, 1)
@@ -342,18 +500,70 @@
         def _():
             u_ref[...] = u_ref[...] + dz[it, pl.ds(1, CX)]
 
-
-def relaxed(source, levels, rows, columns, depth):
+    for q in range(4):
+        block = jnp.transpose(u_ref[pl.ds(4 * q, 4)].reshape(256, NZ))
+        for n, piece in enumerate(chop(block, 2)):
+            ut[pl.ds(256 * n, 256), pl.ds(256 * q, 256)] = piece.astype(BF16)
+
+    @pl.loop(0, NB // 4)
+    def _(c):
+        cell = slot[pl.ds(c, 1), :]
+        a = hot(fit(CX * CY, cell // NZ))
+        v = jnp.dot(ut[...], a, preferred_element_type=F32)
+        v = jnp.where(fit(NZ, cell % NZ), v[:NZ] + v[NZ:], 0.0)
+        smp[pl.ds(c, 1), :] = jnp.sum(v, axis=0, keepdims=True)
+
+    v = smp[...]
+    v = jnp.concatenate([v[:, : 2 * CAP], v[:, 2 * CAP :]], axis=0)
+    v = jnp.concatenate([v[:, :CAP], v[:, CAP:]], axis=0)
+    v = jnp.concatenate([v, jnp.zeros((NB, 128 - CAP), F32)], axis=1)
+    back1[...] = v.reshape(NJ, NI, 128)
+
+    copies = []
+    for t in range(NJ):
+        j = (by + t) % NJ
+        src, dst = back1.at[j], got1.at[pl.ds(al(by, 16), 16)]
+        if t:
+            copies.append(remote(src, dst, gs.at[t], gr.at[t], (bx, j)))
+        else:
+            copies.append(pltpu.make_async_copy(src, dst, gs.at[0]))
+        copies[-1].start()
+    for c in copies:
+        c.wait()
+    for k in range(NI):
+        back2[k] = got1[pl.ds(k, NJ, stride=NI), :]
+    copies = []
+    for t in range(NI):
+        k = bx_peer(bx, t)
+        src, dst = back2.at[k], got2.at[pl.ds(al(bx, 8), 8)]
+        if t:
+            copies.append(remote(src, dst, ks.at[t], kr.at[t], (k, by)))
+        else:
+            copies.append(pltpu.make_async_copy(src, dst, ks.at[0]))
+        copies[-1].start()
+    for c in copies:
+        c.wait()
+    found = [p.astype(BF16) for p in chop(jnp.transpose(got2[...])[:CAP], 3)]
+
+    @pl.loop(0, P_DEV // 256)
+    def _(c):
+        at = pl.ds(al(c, 256), 256)
+        ones = hot(fit(NB, own[:, at]))
+        v = sum(jnp.dot(p, ones, preferred_element_type=F32) for p in found)
+        imp_ref[:, at] = jnp.sum(jnp.where(fit(CAP, rank[:, at]), v, 0.0), axis=0, keepdims=True)
+
+
+def local(normals, owners, cells, levels, rows, columns, depth):
     vm = pl.BlockSpec(memory_space=pltpu.VMEM)
     brick = (CX, CY, NZ)
     tall = (ITERS, CX + 2, CY, NZ)
     dma = pltpu.SemaphoreType.DMA
-    return pl.pallas_call(
+    iterate, implicit = pl.pallas_call(
         relax,
         name="relax",
-        out_shape=jax.ShapeDtypeStruct(brick, F32),
-        in_specs=[vm, pl.BlockSpec(memory_space=pltpu.SMEM), vm, vm, vm],
-        out_specs=vm,
+        out_shape=(jax.ShapeDtypeStruct(brick, F32), jax.ShapeDtypeStruct((1, P_DEV), F32)),
+        in_specs=[vm, vm, vm, pl.BlockSpec(memory_space=pltpu.SMEM), vm, vm, vm],
+        out_specs=(vm, vm),
         scratch_shapes=[
             pltpu.VMEM(brick, F32),
             pltpu.VMEM((ITERS, NI * CX, 8, 128), F32),
@@ -372,84 +582,36 @@
             pltpu.VMEM((2, 256, 256), BF16),
             pltpu.VMEM((2, 512, 512), BF16),
             pltpu.VMEM((2, 256, 256), BF16),
+            pltpu.VMEM((2, NB, 128), F32),
+            pltpu.VMEM((1, P_DEV), jnp.int32),
+            pltpu.VMEM((2, NB, 128), F32),
+            pltpu.VMEM((NJ, 2, NI, 128), F32),
+            pltpu.VMEM((NJ, 2, NI, 128), F32),
+            pltpu.VMEM((NB // 4, 256), jnp.int32),
+            pltpu.VMEM((6, NB // 4, 256), F32),
+            pltpu.VMEM((CX + 2, CY, NZ), F32),
+            pltpu.VMEM(brick, F32),
+            pltpu.VMEM(brick, F32),
+            pltpu.VMEM((2, CX, NZ), F32),
+            pltpu.VMEM((2, CX, NZ), F32),
+            pltpu.VMEM((NB // 4, 256), F32),
+            pltpu.VMEM((512, CX * CY), BF16),
+            pltpu.VMEM((NJ, NI, 128), F32),
+            pltpu.VMEM((NB, 128), F32),
+            pltpu.VMEM((NI, NJ, 128), F32),
+            pltpu.VMEM((NB, 128), F32),
             dma((NI,)), dma((NI,)), dma((NI,)), dma((NI,)),
             dma((2, NI)), dma((2, 2)),
             dma((NJ,)), dma((NJ,)), dma((NJ,)), dma((NJ,)), dma((NJ,)), dma((NJ,)),
             dma((2,)), dma((2,)), dma((4,)), dma((4,)),
+            dma((NI,)), dma((NI,)), dma((NJ,)), dma((NJ,)), dma((4,)), dma((4,)),
+            dma((NJ,)), dma((NJ,)), dma((NI,)), dma((NI,)),
         ],
         compiler_params=pltpu.CompilerParams(
             collective_id=0, has_side_effects=True, vmem_limit_bytes=52 << 20
         ),
-    )(source, levels, rows, columns, depth)
-
-
-screen_base = 1.0
-
-
-def padded(shard, sides, width):
-    for axis, dim in sides:
-        peers, length = (lax.axis_size(axis), shard.shape[dim])
-        up = [(i, (i + 1) % peers) for i in range(peers - 1)]
-        down = [(j, i) for i, j in up]
-        last = lax.slice_in_dim(shard, length - width, length, axis=dim)
-        initial = lax.slice_in_dim(shard, 0, width, axis=dim)
-        before = lax.ppermute(last, axis, up)
-        after = lax.ppermute(initial, axis, down)
-        shard = jnp.concatenate([before, shard, after], axis=dim)
-    return shard
-
-
-def local(normals, owners, cells, levels, rows_inverse, columns_inverse, depth_inverse):
-    first_count = lax.axis_size("bx")
-    second_count = lax.axis_size("by")
-    bricks = first_count * second_count
-    point_count = cells.shape[0]
-    capacity = 2 * point_count // bricks
-    brick_cells = CX * CY * NZ
-    target = owners[:, 0]
-    onehot = (target[:, None] == jnp.arange(bricks, dtype=jnp.int32)[None, :]).astype(jnp.int32)
-    ranking = jnp.sum(onehot * (jnp.cumsum(onehot, axis=0) - 1), axis=1)
-    slot_index = target * capacity + ranking
-    send_normals = jnp.zeros((3, bricks * capacity), jnp.float32).at[:, slot_index].set(normals)
-    send_cells = jnp.zeros((bricks * capacity,), jnp.int32).at[slot_index].set(cells)
-    arrived_normals, arrived_cells = (
-        lax.all_to_all(
-            send_normals.reshape(3, bricks, capacity),
-            ("bx", "by"),
-            split_axis=1,
-            concat_axis=1,
-            tiled=True,
-        ),
-        lax.all_to_all(
-            send_cells.reshape(1, bricks, capacity),
-            ("bx", "by"),
-            split_axis=1,
-            concat_axis=1,
-            tiled=True,
-        ),
-    )
-    flat_cells = arrived_cells.reshape(-1)
-    vector_field = (
-        jnp.zeros((3, brick_cells), jnp.float32)
-        .at[:, flat_cells]
-        .add(arrived_normals.reshape(3, -1))
-    )
-    vector_field = vector_field.reshape(3, CX, CY, NZ)
-    stretched = padded(vector_field, (("bx", 1), ("by", 2)), 1)
-    z_padded = jnp.pad(vector_field[2], ((0, 0), (0, 0), (1, 1)))
-    source = -0.5 * (
-        stretched[0, 2:, 1:-1]
-        - stretched[0, :-2, 1:-1]
-        + (stretched[1, 1:-1, 2:] - stretched[1, 1:-1, :-2])
-        + (z_padded[:, :, 2:] - z_padded[:, :, :-2])
-    )
-    iterate = relaxed(source, levels, rows_inverse, columns_inverse, depth_inverse)
-    sampled = iterate.reshape(-1)[flat_cells]
-    returned = lax.all_to_all(
-        sampled.reshape(1, bricks, capacity), ("bx", "by"), split_axis=1, concat_axis=1, tiled=True
-    )
-    implicit = returned.reshape(-1)[slot_index]
-    return (iterate, implicit)
+    )(normals, owners.reshape(1, P_DEV), cells.reshape(1, P_DEV), levels, rows, columns, depth)
+    return iterate, implicit.reshape(P_DEV)
 
 
 def solution(mesh):

time: 831 us -> 394 us (0.47)
  local copies, waits for them, and re-layouts: 283 us -> 5.74 us
  other arithmetic: 176 us -> 0 us
  Pallas kernels: 304 us -> 387 us
  starting transfers between devices: 44.9 us -> 0 us
  waiting for transfers between devices: 13.6 us -> 0 us
    scatter-add x3 -> x0, other arithmetic: 166 us -> none  [local(): vector_field = jnp.zeros((3, brick_cells), jnp.float32).at[:, flat_cells]...]
    gather x2 -> x0, local copies, waits for them, and re-layouts: 86.1 us -> none  [the longest x1 45.5 us: local(): sampled = iterate.reshape(-1)[flat_cells]]
    pallas_call x1, Pallas kernels: 304 us -> 387 us  [local(): pl.pallas_call(relax, name='relax', out_shape=(jax.ShapeDtypeStruct(brick...]
    reshape x8 -> x0, local copies, waits for them, and re-layouts: 83.3 us -> none  [the longest x1 76 us: local(): vector_field = vector_field.reshape(3, CX, CY, NZ)]
    slice x2 -> x0, local copies, waits for them, and re-layouts: 75.8 us -> none  [the longest x1 75.7 us: local(): z_padded = jnp.pad(vector_field[2], ((0, 0), (0, 0), (1, 1)))]
    all_to_all x3 -> x0, starting transfers between devices: 32.4 us -> none  [the longest x1 11.5 us: local(): lax.all_to_all(send_cells.reshape(1, bricks, capacity), ('bx', 'by'), spl...]
    scatter x2 -> x0, local copies, waits for them, and re-layouts: 28.5 us -> none  [the longest x1 15.7 us: local(): jnp.zeros((bricks * capacity,), jnp.int32).at[slot_index].set(cells)]
    ppermute x4 -> x0, starting transfers between devices: 12.5 us -> none  [the longest x2 9.31 us: padded(): before = lax.ppermute(last, axis, up)]
  transfers between devices with their start and end apart: 7 -> 0, of which waited for: 4 -> 0; matrix products, arithmetic and copies ran while one was open for 13% -> 0% of each run, Pallas kernels for 0% -> 0%
where the time goes in v2:
time: 394 us
  Pallas kernels  387 us (98%)
  local copies, waits for them, and re-layouts  5.74 us (1%)
    pallas_call x1, Pallas kernels, local(): pl.pallas_call(relax, name='relax', out_shape=(jax.ShapeDtypeStruct(brick...  387 us

profile of v2, /device:TPU:1, one launch (start us, length us, event | category | flops | bytes accessed | tf_op | source)
XLA Modules:
  0.0 394.0 jit_solution(684042882893904118)
XLA Ops:
  1.3 0.0 copy-start
  1.3 0.9 copy-done
  2.2 0.0 copy-start.1
  2.2 0.9 copy-done.1
  3.2 0.0 copy-start.2
  3.2 0.8 copy-done.2
  4.0 0.0 copy-start.3
  4.0 0.7 copy-done.3
  4.7 0.0 copy-start.4
  4.7 0.7 copy-done.4
  5.5 387.0 %relax.1 = (f32[16,64,256]{2,1,0:T(8,128)S(1)}, f32[1,4096]{1,0:T(1,128)S(1)}) custom-call(f32[3,4096]{1,0:T(4,128)S(1)} %copy-done.2, s32[1,4096]{1,0:T(1,128)S(1)} %bitcast.3, s32[1,4096]{1,0:T(1,128)S(1)} %bitcast.4, s32[1,1]{1,0:T(1,128)S(6)} %copy.11.lev_ref, f32[256,256]{1,0:T(8,128)S(1)} %copy-done, f32[512,512]{1,0:T(8,128)} %my_ref.1, ...), custom_call_target="tpu_custom_call" | custom-call | tf_op jit(solution)/shard_map/relax/pallas_call | solution.py:561
  392.5 1.0 copy.12
  393.4 0.6 copy.13
Async XLA Ops:
  1.3 1.0 copy-start
  2.2 0.9 copy-start.1
  3.2 0.8 copy-start.2
  4.0 0.7 copy-start.3
  4.7 0.7 copy-start.4

commit v3 on v2

--- a/solution.py
+++ b/solution.py
@@ -52,16 +52,16 @@
     for t in range(2, NJ - 1):
         pl.semaphore_signal(barrier, inc=1, device_id=(bx, (by + t) % NJ), device_id_type=MESH)
         count += 1
-    pl.semaphore_wait(barrier, count)
+    return functools.partial(pl.semaphore_wait, barrier, count)
 
 
 def relax(
     nrm, own, cel, lev_ref, mx_ref, my_ref, mz_ref, u_ref, imp_ref,
     r, xin, dxp, dx, edge, yhx, yin, dyl, dy, ye, yhy, dz, ze, yhz,
-    mxs, mys, mzs,
-    box, rank, in1, out2, in2, slot, part, vx, vy, vz, fe, fh, smp, ut, back1, got1, back2, got2,
+    mxv, myv, mzv, mxs, mys, mzs,
+    box, rank, in1, out2, in2, slot, vx, vy, vz, fe, fh, ut, back1, got1, back2, got2,
     xs, xr, bs, br, es, er, ys, yr, cs, cr, ns, nr, hs, hr, zs, zr,
-    ps, pr, qs, qr, fs, fr, gs, gr, ks, kr,
+    ps, pr, qs, qr, fs, fr, gs, gr, ks, kr, ms,
 ):
     bx, by = lax.axis_index("bx"), lax.axis_index("by")
     yg, zh = bx // 2, bx % 2
@@ -77,14 +77,19 @@
             ref[it, CX + 1] = jnp.zeros((CY, NZ), F32)
     vx[0] = jnp.zeros((CY, NZ), F32)
     vx[CX + 1] = jnp.zeros((CY, NZ), F32)
+    fh[...] = jnp.zeros(fh.shape, F32)
+    back1[...] = jnp.zeros(back1.shape, F32)
+    all_here = greet(bx, by)
+    fetches = [
+        pltpu.make_async_copy(m, v, ms.at[n])
+        for n, (m, v) in enumerate(((mx_ref, mxv), (my_ref, myv), (mz_ref, mzv)))
+    ]
+    for c in fetches:
+        c.start()
     vx[pl.ds(1, CX)] = jnp.zeros((CX, CY, NZ), F32)
     vy[...] = jnp.zeros(vy.shape, F32)
     vz[...] = jnp.zeros(vz.shape, F32)
-    fh[...] = jnp.zeros(fh.shape, F32)
     u_ref[...] = jnp.zeros(u_ref.shape, F32)
-    for m, ms in ((mx_ref, mxs), (my_ref, mys), (mz_ref, mzs)):
-        ms[0], ms[1] = split(m[...])
-    greet(bx, by)
     below, above = jnp.maximum(by - 1, 0), jnp.minimum(by + 1, NJ - 1)
     lanes = (((1,), (1,)), ((), ()))
 
@@ -125,6 +130,7 @@
 
     lax.fori_loop(0, P_DEV // 256, dispatch, jnp.zeros((NB, 256), F32))
 
+    all_here()
     copies = []
     for t in range(NI):
         k = bx_peer(bx, t)
@@ -145,31 +151,27 @@
         if t:
             copies.append(remote(out2.at[j], in2.at[by], qs.at[t], qr.at[t], (bx, j)))
         else:
-            copies.append(pltpu.make_async_copy(out2.at[j], in2.at[by], qs.at[0]))
+            copies.append(pltpu.make_async_copy(out2.at[j], in2.at[by], qr.at[0]))
         copies[-1].start()
-    for c in copies:
+    for c, (v, vs) in zip(fetches, ((mxv, mxs), (myv, mys), (mzv, mzs))):
         c.wait()
-
-    for k in range(4):
-        v = in2[:, k // 2].reshape(NB, 128)[:, CAP * (k % 2) : CAP * (k % 2 + 1)]
-        v = jnp.concatenate([v[: NB // 2], v[NB // 2 :]], axis=1)
-        v = jnp.concatenate([v[: NB // 4], v[NB // 4 :]], axis=1)
-        if k < 3:
-            part[2 * k], part[2 * k + 1] = chop(v, 2)
-        else:
-            slot[...] = v.astype(jnp.int32)
-
-    @pl.loop(0, NB // 4)
-    def _(c):
-        cell = slot[pl.ds(c, 1), :]
+        vs[0], vs[1] = split(v[...])
+
+    @pl.loop(0, NJ)
+    def _(t):
+        j = (by + NJ - t) % NJ
+        remote(out2.at[0], in2.at[j], qs.at[0], qr.at[t], (bx, by)).wait_recv()
+        rows = []
+        for k in range(4):
+            v = in2[j, k // 2][:, CAP * (k % 2) : CAP * (k % 2 + 1)]
+            rows.append(jnp.concatenate([v[i : i + 1] for i in range(NI)], axis=1))
+        cell = rows[3].astype(jnp.int32)
+        slot[pl.ds(j, 1), :] = cell
         depth = fit(NZ, cell % NZ)
         weighted = jnp.concatenate(
             [
-                jnp.concatenate(
-                    [jnp.where(depth, part[2 * k + n, pl.ds(c, 1), :], 0.0).astype(BF16) for n in range(2)],
-                    axis=1,
-                )
-                for k in range(3)
+                jnp.concatenate([jnp.where(depth, p, 0.0).astype(BF16) for p in chop(v, 2)], axis=1)
+                for v in rows[:3]
             ],
             axis=0,
         )
@@ -182,6 +184,9 @@
             vy[pl.ds(4 * q, 4)] += d[:, :, NZ : 2 * NZ]
             vz[pl.ds(4 * q, 4)] += d[:, :, 2 * NZ :]
 
+    for c in copies[1:]:
+        c.wait_send()
+
     down = remote(vx.at[1], vx.at[CX + 1], fs.at[0], fr.at[0], (jnp.maximum(bx - 1, 0), by))
     up = remote(vx.at[CX], vx.at[0], fs.at[1], fr.at[1], (jnp.minimum(bx + 1, NI - 1), by))
     for x in range(CX):
@@ -240,19 +245,17 @@
 
     diagonal = 6.0 + (1.0 + lev_ref[0, 0].astype(F32))
 
-    def stencil(d, low, high):
-        @pl.loop(0, CX)
-        def _(x):
-            c = d[x + 1]
-            zi = lax.broadcasted_iota(jnp.int32, (CY, NZ), 1)
-            yi = lax.broadcasted_iota(jnp.int32, (CY, NZ), 0)
-            near = d[x] + d[x + 2]
-            near = near + jnp.where(zi == 0, 0.0, pltpu.roll(c, 1, 1))
-            near = near + jnp.where(zi == NZ - 1, 0.0, pltpu.roll(c, NZ - 1, 1))
-            near = near + jnp.where(yi == 0, low(x), pltpu.roll(c, 1, 0))
-            near = near + jnp.where(yi == CY - 1, high(x), pltpu.roll(c, CY - 1, 0))
-            r[x] = r[x] - (diagonal * c - near)
-            u_ref[x] = u_ref[x] + c
+    def plane(d, x, low=None, high=None):
+        c = d[x + 1]
+        zi = lax.broadcasted_iota(jnp.int32, (CY, NZ), 1)
+        yi = lax.broadcasted_iota(jnp.int32, (CY, NZ), 0)
+        near = d[x] + d[x + 2]
+        near = near + jnp.where(zi == 0, 0.0, pltpu.roll(c, 1, 1))
+        near = near + jnp.where(zi == NZ - 1, 0.0, pltpu.roll(c, NZ - 1, 1))
+        near = near + jnp.where(yi == 0, low(x) if low else 0.0, pltpu.roll(c, 1, 0))
+        near = near + jnp.where(yi == CY - 1, high(x) if high else 0.0, pltpu.roll(c, CY - 1, 0))
+        r[x] = r[x] - (diagonal * c - near)
+        u_ref[x] = u_ref[x] + c
 
     def x_planes(d, send, recv):
         down = remote(d.at[1], d.at[CX + 1], send.at[0], recv.at[0], (jnp.maximum(bx - 1, 0), by))
@@ -351,15 +354,16 @@
             half(1, 0).wait_recv()
             half(1, 1).wait_recv()
 
-        stencil(
-            dx.at[it],
-            lambda x: yhx[it, 1, pl.ds(x, 1), :],
-            lambda x: yhx[it, 0, pl.ds(x, 1), :],
-        )
-
         copies = []
-        for t in range(NJ):
+        for t in [*range(1, NJ), 0]:
             j = (by + t) % NJ
+            for e in range(2):
+                plane(
+                    dx.at[it],
+                    2 * j + e,
+                    lambda x: yhx[it, 1, pl.ds(x, 1), :],
+                    lambda x: yhx[it, 0, pl.ds(x, 1), :],
+                )
             src = r.at[pl.ds(2 * j, 2)]
             dst = yin.at[it, :, pl.ds(al(by, 64), 64), :]
             if t:
@@ -416,6 +420,12 @@
             copies[2 * t + 1].wait()
         copies[1].wait()
 
+        rows = (lambda x: yhy[it, x // 2, pl.ds(x % 2, 1), :], lambda x: yhy[it, x // 2, pl.ds(2 + x % 2, 1), :])
+
+        @pl.loop(1, CX - 1)
+        def _(x):
+            plane(dy.at[it], x, *rows)
+
         @pl.when(bx > 0)
         def _():
             down.wait_send()
@@ -426,12 +436,8 @@
             up.wait_send()
             down.wait_recv()
 
-        stencil(
-            dy.at[it],
-            lambda x: yhy[it, x // 2, pl.ds(x % 2, 1), :],
-            lambda x: yhy[it, x // 2, pl.ds(2 + x % 2, 1), :],
-        )
-
+        for x in (0, CX - 1):
+            plane(dy.at[it], x, *rows)
 
         def z_planes(x, n):
             v = r[pl.ds(x, n)].reshape(n * CY, NZ)
@@ -441,6 +447,8 @@
         z_planes(0, 1)
         z_planes(CX - 1, 1)
         down, up = x_planes(dz.at[it], zs, zr)
+        low = remote(ze.at[0], yhz.at[it, 0], zs.at[2], zr.at[2], (bx, below))
+        high = remote(ze.at[1], yhz.at[it, 1], zs.at[3], zr.at[3], (bx, above))
         more = it < ITERS - 1
 
         @pl.when(more & (bx > 0))
@@ -450,25 +458,43 @@
         @pl.when(more & (bx < NI - 1))
         def _():
             up.start()
+
+        outer = jnp.concatenate(
+            [r[x, y : y + 1, :] for y in (0, CY - 1) for x in range(CX)], axis=0
+        )
+        outer = dot3(*split(outer), mzs[0], mzs[1], lanes)
+        ze[0] = outer[:CX]
+        ze[1] = outer[CX:]
+
+        @pl.when(more & (by > 0))
+        def _():
+            low.start()
+
+        @pl.when(more & (by < NJ - 1))
+        def _():
+            high.start()
 
         for x in range(1, CX - 1, 2):
             z_planes(x, 2)
 
         @pl.when(more)
         def _():
-            for x in range(CX):
-                ze[0, x : x + 1] = dz[it, x + 1, 0:1]
-                ze[1, x : x + 1] = dz[it, x + 1, CY - 1 : CY]
-            low = remote(ze.at[0], yhz.at[it, 0], zs.at[2], zr.at[2], (bx, below))
-            high = remote(ze.at[1], yhz.at[it, 1], zs.at[3], zr.at[3], (bx, above))
-
-            @pl.when(by > 0)
+            @pl.loop(1, CX - 1)
+            def _(x):
+                plane(dz.at[it], x)
+
+            @pl.when(bx > 0)
             def _():
-                low.start()
-
-            @pl.when(by < NJ - 1)
+                down.wait_send()
+                up.wait_recv()
+
+            @pl.when(bx < NI - 1)
             def _():
-                high.start()
+                up.wait_send()
+                down.wait_recv()
+
+            for x in (0, CX - 1):
+                plane(dz.at[it], x)
 
             @pl.when(by > 0)
             def _():
@@ -480,21 +506,9 @@
                 high.wait_send()
                 low.wait_recv()
 
-            @pl.when(bx > 0)
-            def _():
-                down.wait_send()
-                up.wait_recv()
-
-            @pl.when(bx < NI - 1)
-            def _():
-                up.wait_send()
-                down.wait_recv()
-
-            stencil(
-                dz.at[it],
-                lambda x: yhz[it, 1, pl.ds(x, 1), :],
-                lambda x: yhz[it, 0, pl.ds(x, 1), :],
-            )
+            for x in range(CX):
+                r[x, 0:1] += yhz[it, 1, x : x + 1, :]
+                r[x, CY - 1 : CY] += yhz[it, 0, x : x + 1, :]
 
         @pl.when(it == ITERS - 1)
         def _():
@@ -505,31 +519,30 @@
         for n, piece in enumerate(chop(block, 2)):
             ut[pl.ds(256 * n, 256), pl.ds(256 * q, 256)] = piece.astype(BF16)
 
-    @pl.loop(0, NB // 4)
-    def _(c):
-        cell = slot[pl.ds(c, 1), :]
+    def returned(j, t):
+        return remote(back1.at[j], got1.at[pl.ds(al(by, 16), 16)], gs.at[t], gr.at[t], (bx, j))
+
+    def sampled(t):
+        j = (by + t) % NJ
+        cell = slot[pl.ds(j, 1), :]
         a = hot(fit(CX * CY, cell // NZ))
         v = jnp.dot(ut[...], a, preferred_element_type=F32)
         v = jnp.where(fit(NZ, cell % NZ), v[:NZ] + v[NZ:], 0.0)
-        smp[pl.ds(c, 1), :] = jnp.sum(v, axis=0, keepdims=True)
-
-    v = smp[...]
-    v = jnp.concatenate([v[:, : 2 * CAP], v[:, 2 * CAP :]], axis=0)
-    v = jnp.concatenate([v[:, :CAP], v[:, CAP:]], axis=0)
-    v = jnp.concatenate([v, jnp.zeros((NB, 128 - CAP), F32)], axis=1)
-    back1[...] = v.reshape(NJ, NI, 128)
-
-    copies = []
-    for t in range(NJ):
-        j = (by + t) % NJ
-        src, dst = back1.at[j], got1.at[pl.ds(al(by, 16), 16)]
-        if t:
-            copies.append(remote(src, dst, gs.at[t], gr.at[t], (bx, j)))
-        else:
-            copies.append(pltpu.make_async_copy(src, dst, gs.at[0]))
-        copies[-1].start()
-    for c in copies:
-        c.wait()
+        v = jnp.sum(v, axis=0, keepdims=True)
+        for i in range(NI):
+            back1[j, i : i + 1, :CAP] = v[:, CAP * i : CAP * (i + 1)]
+
+    @pl.loop(1, NJ)
+    def _(t):
+        sampled(t)
+        returned((by + t) % NJ, t).start()
+
+    sampled(0)
+    mine = pltpu.make_async_copy(back1.at[by], got1.at[pl.ds(al(by, 16), 16)], gs.at[0])
+    mine.start()
+    for t in range(1, NJ):
+        returned((by + t) % NJ, t).wait()
+    mine.wait()
     for k in range(NI):
         back2[k] = got1[pl.ds(k, NJ, stride=NI), :]
     copies = []
@@ -555,6 +568,7 @@
 
 def local(normals, owners, cells, levels, rows, columns, depth):
     vm = pl.BlockSpec(memory_space=pltpu.VMEM)
+    hb = pl.BlockSpec(memory_space=pl.ANY)
     brick = (CX, CY, NZ)
     tall = (ITERS, CX + 2, CY, NZ)
     dma = pltpu.SemaphoreType.DMA
@@ -562,7 +576,7 @@
         relax,
         name="relax",
         out_shape=(jax.ShapeDtypeStruct(brick, F32), jax.ShapeDtypeStruct((1, P_DEV), F32)),
-        in_specs=[vm, vm, vm, pl.BlockSpec(memory_space=pltpu.SMEM), vm, vm, vm],
+        in_specs=[vm, vm, vm, pl.BlockSpec(memory_space=pltpu.SMEM), hb, hb, hb],
         out_specs=(vm, vm),
         scratch_shapes=[
             pltpu.VMEM(brick, F32),
@@ -579,6 +593,9 @@
             pltpu.VMEM(tall, F32),
             pltpu.VMEM((2, CX, NZ), F32),
             pltpu.VMEM((ITERS, 2, CX, NZ), F32),
+            pltpu.VMEM((256, 256), F32),
+            pltpu.VMEM((512, 512), F32),
+            pltpu.VMEM((256, 256), F32),
             pltpu.VMEM((2, 256, 256), BF16),
             pltpu.VMEM((2, 512, 512), BF16),
             pltpu.VMEM((2, 256, 256), BF16),
@@ -587,14 +604,12 @@
             pltpu.VMEM((2, NB, 128), F32),
             pltpu.VMEM((NJ, 2, NI, 128), F32),
             pltpu.VMEM((NJ, 2, NI, 128), F32),
-            pltpu.VMEM((NB // 4, 256), jnp.int32),
-            pltpu.VMEM((6, NB // 4, 256), F32),
+            pltpu.VMEM((NJ, NI * CAP), jnp.int32),
             pltpu.VMEM((CX + 2, CY, NZ), F32),
             pltpu.VMEM(brick, F32),
             pltpu.VMEM(brick, F32),
             pltpu.VMEM((2, CX, NZ), F32),
             pltpu.VMEM((2, CX, NZ), F32),
-            pltpu.VMEM((NB // 4, 256), F32),
             pltpu.VMEM((512, CX * CY), BF16),
             pltpu.VMEM((NJ, NI, 128), F32),
             pltpu.VMEM((NB, 128), F32),
@@ -605,7 +620,7 @@
             dma((NJ,)), dma((NJ,)), dma((NJ,)), dma((NJ,)), dma((NJ,)), dma((NJ,)),
             dma((2,)), dma((2,)), dma((4,)), dma((4,)),
             dma((NI,)), dma((NI,)), dma((NJ,)), dma((NJ,)), dma((4,)), dma((4,)),
-            dma((NJ,)), dma((NJ,)), dma((NI,)), dma((NI,)),
+            dma((NJ,)), dma((NJ,)), dma((NI,)), dma((NI,)), dma((3,)),
         ],
         compiler_params=pltpu.CompilerParams(
             collective_id=0, has_side_effects=True, vmem_limit_bytes=52 << 20

time: 394 us -> 355 us (0.901)
  Pallas kernels: 387 us -> 348 us
    pallas_call x1, Pallas kernels: 387 us -> 348 us  [local(): pl.pallas_call(relax, name='relax', out_shape=(jax.ShapeDtypeStruct(brick...]
where the time goes in v3:
time: 355 us
  Pallas kernels  348 us (98%)
  local copies, waits for them, and re-layouts  5.74 us (2%)
    pallas_call x1, Pallas kernels, local(): pl.pallas_call(relax, name='relax', out_shape=(jax.ShapeDtypeStruct(brick...  348 us

profile of v3, /device:TPU:1, one launch (start us, length us, event | category | flops | bytes accessed | tf_op | source)
XLA Modules:
  0.0 354.6 jit_solution(12949288796734849129)
XLA Ops:
  1.3 0.0 copy-start
  1.3 0.9 copy-done
  2.2 0.0 copy-start.1
  2.2 0.9 copy-done.1
  3.2 0.0 copy-start.2
  3.2 0.8 copy-done.2
  4.0 0.0 copy-start.3
  4.0 0.7 copy-done.3
  4.7 0.0 copy-start.4
  4.7 0.7 copy-done.4
  5.5 347.5 %relax.1 = (f32[16,64,256]{2,1,0:T(8,128)S(1)}, f32[1,4096]{1,0:T(1,128)S(1)}) custom-call(f32[3,4096]{1,0:T(4,128)S(1)} %copy-done.2, s32[1,4096]{1,0:T(1,128)S(1)} %bitcast.3, s32[1,4096]{1,0:T(1,128)S(1)} %bitcast.4, s32[1,1]{1,0:T(1,128)S(6)} %copy.11.lev_ref, f32[256,256]{1,0:T(8,128)S(1)} %copy-done, f32[512,512]{1,0:T(8,128)} %my_ref.1, ...), custom_call_target="tpu_custom_call" | custom-call | tf_op jit(solution)/shard_map/relax/pallas_call | solution.py:575
  353.0 1.0 copy.12
  354.0 0.6 copy.13
Async XLA Ops:
  1.3 1.0 copy-start
  2.2 0.9 copy-start.1
  3.2 0.8 copy-start.2
  4.0 0.7 copy-start.3
  4.7 0.7 copy-start.4

commit v4 on v3

--- a/solution.py
+++ b/solution.py
@@ -32,6 +32,9 @@
 def bx_peer(bx, t):
     y, z = bx // 4, bx % 4
     return ((y + t // 4) % 4) * 4 + (z + t % 4) % 4
+
+
+BX_ORDER = (5, 10, 15, 1, 6, 11, 12, 2, 7, 8, 13, 3, 4, 9, 14, 0)
 
 
 def al(v, m):
@@ -264,41 +267,20 @@
 
     @pl.loop(0, ITERS)
     def _(it):
-        copies = []
-        for t in range(NI):
-            k = bx_peer(bx, t)
-            src = r.at[:, pl.ds(al(k // 2, 8), 8), pl.ds(al(k % 2, 128), 128)]
-            dst = xin.at[it, pl.ds(bx * 16, 16)]
-            if t:
-                copies.append(remote(src, dst, xs.at[t], xr.at[t], (k, by)))
-            else:
-                copies.append(pltpu.make_async_copy(src, dst, xs.at[0]))
-            copies[-1].start()
-        for c in copies:
-            c.wait()
+        there = []
+        for h in range(2):
+            for t in BX_ORDER:
+                k = bx_peer(bx, t)
+                src = r.at[:, pl.ds(al(2 * (k // 2) + h, 4), 4), pl.ds(al(k % 2, 128), 128)]
+                dst = xin.at[it, pl.ds(bx * 16, 16), pl.ds(4 * h, 4)]
+                if t:
+                    there.append(remote(src, dst, xs.at[h, t], xr.at[h, t], (k, by)))
+                else:
+                    there.append(pltpu.make_async_copy(src, dst, xs.at[h, 0]))
+                there[-1].start()
         lines = xin.at[it].reshape(NI * CX * 8, 128)
         moved = dxp.reshape((NI * CX + 2) * 8, 128)
-        for s in range(0, 8, 2):
-            v = jnp.concatenate(
-                [lines[pl.ds(s, 256, stride=8), :], lines[pl.ds(s + 1, 256, stride=8), :]], axis=1
-            )
-            d = dot3(mxs[0], mxs[1], *split(v))
-            moved[pl.ds(8 + s, 256, stride=8), :] = d[:, :128]
-            moved[pl.ds(9 + s, 256, stride=8), :] = d[:, 128:]
-            if s == 0:
-                edge[0] = d[:, :128]
-            if s == 6:
-                edge[1] = d[:, 128:]
         copies = []
-        for t in range(NI):
-            k = bx_peer(bx, t)
-            src = dxp.at[pl.ds(k * 16, 18)]
-            dst = dx.at[it, :, pl.ds(al(yg, 8), 8), pl.ds(al(zh, 128), 128)]
-            if t:
-                copies.append(remote(src, dst, bs.at[t], br.at[t], (k, by)))
-            else:
-                copies.append(pltpu.make_async_copy(src, dst, bs.at[0]))
-            copies[-1].start()
 
         def edges(side, beside):
             out = []
@@ -321,15 +303,41 @@
                 es.at[side, 0], er.at[side, z], (bx, by),
             )
 
-        @pl.when((yg == 0) & (by > 0))
-        def _():
-            for c in edges(0, below):
-                c.start()
-
-        @pl.when((yg == 7) & (by < NJ - 1))
-        def _():
-            for c in edges(1, above):
-                c.start()
+        for h in range(2):
+            for c in there[NI * h : NI * (h + 1)]:
+                c.wait()
+            for y in range(4 * h, 4 * h + 4, 2):
+                v = jnp.concatenate([lines[pl.ds(y + n, 256, stride=8), :] for n in range(2)], axis=1)
+                d = dot3(mxs[0], mxs[1], *split(v))
+                moved[pl.ds(8 + y, 256, stride=8), :] = d[:, :128]
+                moved[pl.ds(9 + y, 256, stride=8), :] = d[:, 128:]
+                if y == 0:
+                    edge[0] = d[:, :128]
+                if y == 6:
+                    edge[1] = d[:, 128:]
+            for t in BX_ORDER:
+                k = bx_peer(bx, t)
+                src = dxp.at[pl.ds(k * 16, 18), pl.ds(4 * h, 4)]
+                dst = dx.at[it, :, pl.ds(al(2 * yg + h, 4), 4), pl.ds(al(zh, 128), 128)]
+                if t:
+                    copies.append(remote(src, dst, bs.at[h, t], br.at[h, t], (k, by)))
+                else:
+                    copies.append(pltpu.make_async_copy(src, dst, bs.at[h, 0]))
+                copies[-1].start()
+
+            if h == 0:
+
+                @pl.when((yg == 0) & (by > 0))
+                def _():
+                    for c in edges(0, below):
+                        c.start()
+
+            else:
+
+                @pl.when((yg == 7) & (by < NJ - 1))
+                def _():
+                    for c in edges(1, above):
+                        c.start()
 
         for c in copies:
             c.wait()
@@ -353,6 +361,13 @@
         def _():
             half(1, 0).wait_recv()
             half(1, 1).wait_recv()
+
+        def there(j, t, h):
+            src = r.at[pl.ds(2 * j, 2), :, pl.ds(128 * h, 128)]
+            dst = yin.at[it, h, :, pl.ds(al(by, 64), 64), :]
+            if t:
+                return remote(src, dst, ys.at[h, t], yr.at[h, t], (bx, j))
+            return pltpu.make_async_copy(src, dst, ys.at[h, 0])
 
         copies = []
         for t in [*range(1, NJ), 0]:
@@ -364,41 +379,44 @@
                     lambda x: yhx[it, 1, pl.ds(x, 1), :],
                     lambda x: yhx[it, 0, pl.ds(x, 1), :],
                 )
-            src = r.at[pl.ds(2 * j, 2)]
-            dst = yin.at[it, :, pl.ds(al(by, 64), 64), :]
-            if t:
-                copies.append(remote(src, dst, ys.at[t], yr.at[t], (bx, j)))
-            else:
-                copies.append(pltpu.make_async_copy(src, dst, ys.at[0]))
+            copies.append(there(j, t, 0))
             copies[-1].start()
-        for c in copies:
-            c.wait()
-        for e in range(2):
-            d = dot3(mys[0], mys[1], *split(yin[it, e]))
-            dyl[e] = d
-            for j in range(NJ):
-                if j:
-                    ye[j, e : e + 1] = d[64 * j - 1 : 64 * j]
-                if j < NJ - 1:
-                    ye[j, 2 + e : 3 + e] = d[64 * j + 64 : 64 * j + 65]
-        copies = []
-        for t in range(NJ):
-            j = (by + t) % NJ
-            main = (dyl.at[:, pl.ds(al(j, 64), 64), :], dy.at[it, pl.ds(1 + 2 * by, 2)])
-            rows = (ye.at[j], yhy.at[it, by])
-            if t:
-                copies.append(remote(*main, cs.at[t], cr.at[by], (bx, j)))
-                copies.append(remote(*rows, ns.at[t], nr.at[t], (bx, j)))
-            else:
-                copies.append(pltpu.make_async_copy(*main, cr.at[by]))
-                copies.append(pltpu.make_async_copy(*rows, ns.at[0]))
-            copies[-2].start()
+        for t in [*range(1, NJ), 0]:
+            copies.append(there((by + t) % NJ, t, 1))
             copies[-1].start()
+        for h in range(2):
+            for c in copies[NJ * h : NJ * (h + 1)]:
+                c.wait()
+            d = dot3(mys[0], mys[1], *split(jnp.concatenate([yin[it, h, 0], yin[it, h, 1]], axis=1)))
+            for e in range(2):
+                part = d[:, 128 * e : 128 * (e + 1)]
+                dyl[h, e] = part
+                for j in range(NJ):
+                    if j:
+                        ye[h, j, e : e + 1] = part[64 * j - 1 : 64 * j]
+                    if j < NJ - 1:
+                        ye[h, j, 2 + e : 3 + e] = part[64 * j + 64 : 64 * j + 65]
+            for t in [*range(1, NJ), 0]:
+                j = (by + t) % NJ
+                half_z = pl.ds(128 * h, 128)
+                main = (dyl.at[h, :, pl.ds(al(j, 64), 64), :], dy.at[it, pl.ds(1 + 2 * by, 2), :, half_z])
+                rows = (ye.at[h, j], yhy.at[it, by, :, half_z])
+                if t:
+                    copies.append(remote(*main, cs.at[h, t], cr.at[h, by], (bx, j)))
+                    copies.append(remote(*rows, ns.at[h, t], nr.at[h, t], (bx, j)))
+                else:
+                    copies.append(pltpu.make_async_copy(*main, cr.at[h, by]))
+                    copies.append(pltpu.make_async_copy(*rows, ns.at[h, 0]))
+                copies[-2].start()
+                copies[-1].start()
 
         def arrived(m):
-            remote(
-                dyl.at[:, pl.ds(0, 64), :], dy.at[it, pl.ds(1 + 2 * m, 2)], cs.at[0], cr.at[m], (bx, by)
-            ).wait_recv()
+            for h in range(2):
+                remote(
+                    dyl.at[h, :, pl.ds(0, 64), :],
+                    dy.at[it, pl.ds(1 + 2 * m, 2), :, pl.ds(128 * h, 128)],
+                    cs.at[h, 0], cr.at[h, m], (bx, by),
+                ).wait_recv()
 
         down, up = x_planes(dy.at[it], hs, hr)
         arrived(0)
@@ -415,10 +433,12 @@
 
         for m in range(1, NJ - 1):
             arrived(m)
-        for t in range(1, NJ):
-            copies[2 * t].wait_send()
-            copies[2 * t + 1].wait()
-        copies[1].wait()
+        for h in range(2):
+            back = copies[2 * NJ * (h + 1) : 2 * NJ * (h + 2)]
+            for t in range(NJ - 1):
+                back[2 * t].wait_send()
+                back[2 * t + 1].wait()
+            back[-1].wait()
 
         rows = (lambda x: yhy[it, x // 2, pl.ds(x % 2, 1), :], lambda x: yhy[it, x // 2, pl.ds(2 + x % 2, 1), :])
 
@@ -585,10 +605,10 @@
             pltpu.VMEM(tall, F32),
             pltpu.VMEM((2, NI * CX, 128), F32),
             pltpu.VMEM((ITERS, 2, CX, NZ), F32),
-            pltpu.VMEM((ITERS, 2, NJ * CY, NZ), F32),
-            pltpu.VMEM((2, NJ * CY, NZ), F32),
+            pltpu.VMEM((ITERS, 2, 2, NJ * CY, 128), F32),
+            pltpu.VMEM((2, 2, NJ * CY, 128), F32),
             pltpu.VMEM(tall, F32),
-            pltpu.VMEM((NJ, 8, NZ), F32),
+            pltpu.VMEM((2, NJ, 8, 128), F32),
             pltpu.VMEM((ITERS, NJ, 8, NZ), F32),
             pltpu.VMEM(tall, F32),
             pltpu.VMEM((2, CX, NZ), F32),
@@ -615,15 +635,15 @@
             pltpu.VMEM((NB, 128), F32),
             pltpu.VMEM((NI, NJ, 128), F32),
             pltpu.VMEM((NB, 128), F32),
-            dma((NI,)), dma((NI,)), dma((NI,)), dma((NI,)),
+            dma((2, NI)), dma((2, NI)), dma((2, NI)), dma((2, NI)),
             dma((2, NI)), dma((2, 2)),
-            dma((NJ,)), dma((NJ,)), dma((NJ,)), dma((NJ,)), dma((NJ,)), dma((NJ,)),
+            dma((2, NJ)), dma((2, NJ)), dma((2, NJ)), dma((2, NJ)), dma((2, NJ)), dma((2, NJ)),
             dma((2,)), dma((2,)), dma((4,)), dma((4,)),
             dma((NI,)), dma((NI,)), dma((NJ,)), dma((NJ,)), dma((4,)), dma((4,)),
             dma((NJ,)), dma((NJ,)), dma((NI,)), dma((NI,)), dma((3,)),
         ],
         compiler_params=pltpu.CompilerParams(
-            collective_id=0, has_side_effects=True, vmem_limit_bytes=52 << 20
+            collective_id=0, has_side_effects=True, vmem_limit_bytes=62 << 20
         ),
     )(normals, owners.reshape(1, P_DEV), cells.reshape(1, P_DEV), levels, rows, columns, depth)
     return iterate, implicit.reshape(P_DEV)

time: 355 us -> 322 us (0.907)
  Pallas kernels: 348 us -> 317 us
    pallas_call x1, Pallas kernels: 348 us -> 317 us  [local(): pl.pallas_call(relax, name='relax', out_shape=(jax.ShapeDtypeStruct(brick...]
where the time goes in v4:
time: 322 us; the launch traced here: 321 us
  Pallas kernels  317 us (98%)
    pallas_call x1, Pallas kernels, local(): pl.pallas_call(relax, name='relax', out_shape=(jax.ShapeDtypeStruct(brick...  317 us

profile of v4, /device:TPU:1, one launch (start us, length us, event | category | flops | bytes accessed | tf_op | source)
XLA Modules:
  0.0 321.0 jit_solution(5777253269261430252)
XLA Ops:
  1.3 316.8 %relax.1 = (f32[16,64,256]{2,1,0:T(8,128)}, f32[1,4096]{1,0:T(1,128)}) custom-call(f32[3,4096]{1,0:T(4,128)} %nrm.1, s32[1,4096]{1,0:T(1,128)} %bitcast.3, s32[1,4096]{1,0:T(1,128)} %bitcast.4, s32[1,1]{1,0:T(1,128)S(6)} %copy.11.lev_ref, f32[256,256]{1,0:T(8,128)} %mx_ref.1, f32[512,512]{1,0:T(8,128)} %my_ref.1, f32[256,256]{1,0:T(8,128)} %mz_ref.1), custom_call_target="tpu_custom_call" | custom-call | tf_op jit(solution)/shard_map/relax/pallas_call | solution.py:595
  318.1 0.0 copy-start
  318.1 2.3 copy.12
  320.4 0.0 copy-done
  320.4 0.6 copy.13
Async XLA Ops:
  318.1 2.3 copy-start

commit v5 on v4

--- a/solution.py
+++ b/solution.py
@@ -131,7 +131,7 @@
             box[1] += d[:, 128:]
         return seen + counts[:, 256:]
 
-    lax.fori_loop(0, P_DEV // 256, dispatch, jnp.zeros((NB, 256), F32))
+    lax.fori_loop(0, P_DEV // 256, dispatch, jnp.zeros((NB, 256), F32), unroll=4)
 
     all_here()
     copies = []
@@ -303,6 +303,20 @@
                 es.at[side, 0], er.at[side, z], (bx, by),
             )
 
+        def back(h, part):
+            for t in BX_ORDER:
+                k = bx_peer(bx, t)
+                src = dxp.at[pl.ds(k * 16 + 10 * part, 10 - 2 * part), pl.ds(4 * h, 4)]
+                dst = dx.at[
+                    it, pl.ds(10 * part, 10 - 2 * part), pl.ds(al(2 * yg + h, 4), 4), pl.ds(al(zh, 128), 128)
+                ]
+                n = 2 * part + h
+                if t:
+                    copies.append(remote(src, dst, bs.at[n, t], br.at[n, t], (k, by)))
+                else:
+                    copies.append(pltpu.make_async_copy(src, dst, bs.at[n, 0]))
+                copies[-1].start()
+
         for h in range(2):
             for c in there[NI * h : NI * (h + 1)]:
                 c.wait()
@@ -315,16 +329,7 @@
                     edge[0] = d[:, :128]
                 if y == 6:
                     edge[1] = d[:, 128:]
-            for t in BX_ORDER:
-                k = bx_peer(bx, t)
-                src = dxp.at[pl.ds(k * 16, 18), pl.ds(4 * h, 4)]
-                dst = dx.at[it, :, pl.ds(al(2 * yg + h, 4), 4), pl.ds(al(zh, 128), 128)]
-                if t:
-                    copies.append(remote(src, dst, bs.at[h, t], br.at[h, t], (k, by)))
-                else:
-                    copies.append(pltpu.make_async_copy(src, dst, bs.at[h, 0]))
-                copies[-1].start()
-
+            back(h, 0)
             if h == 0:
 
                 @pl.when((yg == 0) & (by > 0))
@@ -339,18 +344,10 @@
                     for c in edges(1, above):
                         c.start()
 
-        for c in copies:
+        back(0, 1)
+        back(1, 1)
+        for c in copies[: 2 * NI]:
             c.wait()
-
-        @pl.when((yg == 0) & (by > 0))
-        def _():
-            for c in edges(0, below):
-                c.wait_send()
-
-        @pl.when((yg == 7) & (by < NJ - 1))
-        def _():
-            for c in edges(1, above):
-                c.wait_send()
 
         @pl.when(by < NJ - 1)
         def _():
@@ -362,107 +359,130 @@
             half(1, 0).wait_recv()
             half(1, 1).wait_recv()
 
-        def there(j, t, h):
-            src = r.at[pl.ds(2 * j, 2), :, pl.ds(128 * h, 128)]
-            dst = yin.at[it, h, :, pl.ds(al(by, 64), 64), :]
-            if t:
-                return remote(src, dst, ys.at[h, t], yr.at[h, t], (bx, j))
-            return pltpu.make_async_copy(src, dst, ys.at[h, 0])
-
-        copies = []
-        for t in [*range(1, NJ), 0]:
-            j = (by + t) % NJ
-            for e in range(2):
+        forth = []
+        for e in range(2):
+            if e:
+                for c in copies[2 * NI :]:
+                    c.wait()
+            for t in [*range(1, NJ), 0]:
+                j = (by + t) % NJ
                 plane(
                     dx.at[it],
-                    2 * j + e,
+                    j + NJ * e,
                     lambda x: yhx[it, 1, pl.ds(x, 1), :],
                     lambda x: yhx[it, 0, pl.ds(x, 1), :],
                 )
-            copies.append(there(j, t, 0))
-            copies[-1].start()
-        for t in [*range(1, NJ), 0]:
-            copies.append(there((by + t) % NJ, t, 1))
-            copies[-1].start()
-        for h in range(2):
-            for c in copies[NJ * h : NJ * (h + 1)]:
+                src, dst = r.at[j + NJ * e], yin.at[it, e, pl.ds(al(by, 64), 64)]
+                if t:
+                    forth.append(remote(src, dst, ys.at[e, t], yr.at[e, t], (bx, j)))
+                else:
+                    forth.append(pltpu.make_async_copy(src, dst, ys.at[e, 0]))
+                forth[-1].start()
+
+        @pl.when((yg == 0) & (by > 0))
+        def _():
+            for c in edges(0, below):
+                c.wait_send()
+
+        @pl.when((yg == 7) & (by < NJ - 1))
+        def _():
+            for c in edges(1, above):
+                c.wait_send()
+
+        copies = []
+        for e in range(2):
+            for c in forth[NJ * e : NJ * (e + 1)]:
                 c.wait()
-            d = dot3(mys[0], mys[1], *split(jnp.concatenate([yin[it, h, 0], yin[it, h, 1]], axis=1)))
-            for e in range(2):
-                part = d[:, 128 * e : 128 * (e + 1)]
-                dyl[h, e] = part
-                for j in range(NJ):
+            d = dot3(mys[0], mys[1], *split(yin[it, e]))
+            dyl[e] = d
+            for j in range(NJ):
+                for n in range(2):
                     if j:
-                        ye[h, j, e : e + 1] = part[64 * j - 1 : 64 * j]
+                        ye[e, j, n : n + 1] = d[64 * j - 1 : 64 * j, 128 * n : 128 * (n + 1)]
                     if j < NJ - 1:
-                        ye[h, j, 2 + e : 3 + e] = part[64 * j + 64 : 64 * j + 65]
+                        ye[e, j, 2 + n : 3 + n] = d[64 * j + 64 : 64 * j + 65, 128 * n : 128 * (n + 1)]
             for t in [*range(1, NJ), 0]:
                 j = (by + t) % NJ
-                half_z = pl.ds(128 * h, 128)
-                main = (dyl.at[h, :, pl.ds(al(j, 64), 64), :], dy.at[it, pl.ds(1 + 2 * by, 2), :, half_z])
-                rows = (ye.at[h, j], yhy.at[it, by, :, half_z])
+                main = (dyl.at[e, pl.ds(al(j, 64), 64)], dy.at[it, 1 + by + NJ * e])
+                outer = (ye.at[e, j], yhy.at[it, e, by])
                 if t:
-                    copies.append(remote(*main, cs.at[h, t], cr.at[h, by], (bx, j)))
-                    copies.append(remote(*rows, ns.at[h, t], nr.at[h, t], (bx, j)))
+                    copies.append(remote(*main, cs.at[e, t], cr.at[e, by], (bx, j)))
+                    copies.append(remote(*outer, ns.at[e, t], nr.at[e, t], (bx, j)))
                 else:
-                    copies.append(pltpu.make_async_copy(*main, cr.at[h, by]))
-                    copies.append(pltpu.make_async_copy(*rows, ns.at[h, 0]))
+                    copies.append(pltpu.make_async_copy(*main, cr.at[e, by]))
+                    copies.append(pltpu.make_async_copy(*outer, ns.at[e, 0]))
                 copies[-2].start()
                 copies[-1].start()
 
-        def arrived(m):
-            for h in range(2):
-                remote(
-                    dyl.at[h, :, pl.ds(0, 64), :],
-                    dy.at[it, pl.ds(1 + 2 * m, 2), :, pl.ds(128 * h, 128)],
-                    cs.at[h, 0], cr.at[h, m], (bx, by),
-                ).wait_recv()
-
+        def arrived(e, m):
+            remote(
+                dyl.at[e, pl.ds(0, 64)], dy.at[it, 1 + m + NJ * e], cs.at[e, 0], cr.at[e, m], (bx, by)
+            ).wait_recv()
+
+        def rest(e):
+            for n in range(2 * NJ * e, 2 * NJ * (e + 1) - 2, 2):
+                copies[n].wait_send()
+                copies[n + 1].wait()
+            copies[2 * NJ * (e + 1) - 1].wait()
+
+        def outer_row(side):
+            def load(x):
+                at = (it, x // NJ, x % NJ)
+                return jnp.concatenate(
+                    [yhy[(*at, pl.ds(2 * side + n, 1), slice(None))] for n in range(2)], axis=1
+                )
+
+            return load
+
+        rows = (outer_row(0), outer_row(1))
         down, up = x_planes(dy.at[it], hs, hr)
-        arrived(0)
+        arrived(0, 0)
 
         @pl.when(bx > 0)
         def _():
             down.start()
 
-        arrived(NJ - 1)
-
-        @pl.when(bx < NI - 1)
-        def _():
-            up.start()
-
-        for m in range(1, NJ - 1):
-            arrived(m)
-        for h in range(2):
-            back = copies[2 * NJ * (h + 1) : 2 * NJ * (h + 2)]
-            for t in range(NJ - 1):
-                back[2 * t].wait_send()
-                back[2 * t + 1].wait()
-            back[-1].wait()
-
-        rows = (lambda x: yhy[it, x // 2, pl.ds(x % 2, 1), :], lambda x: yhy[it, x // 2, pl.ds(2 + x % 2, 1), :])
-
-        @pl.loop(1, CX - 1)
-        def _(x):
-            plane(dy.at[it], x, *rows)
-
-        @pl.when(bx > 0)
-        def _():
-            down.wait_send()
-            up.wait_recv()
-
-        @pl.when(bx < NI - 1)
-        def _():
-            up.wait_send()
-            down.wait_recv()
-
-        for x in (0, CX - 1):
-            plane(dy.at[it], x, *rows)
+        for m in range(1, NJ):
+            arrived(0, m)
+        rest(0)
 
         def z_planes(x, n):
             v = r[pl.ds(x, n)].reshape(n * CY, NZ)
             d = dot3(*split(v), mzs[0], mzs[1], lanes)
             dz[it, pl.ds(x + 1, n)] = d.reshape(n, CY, NZ)
+
+        @pl.loop(1, NJ - 1)
+        def _(x):
+            plane(dy.at[it], x, *rows)
+
+        for x in range(1, NJ - 1, 2):
+            z_planes(x, 2)
+        arrived(1, NJ - 1)
+
+        @pl.when(bx < NI - 1)
+        def _():
+            up.start()
+
+        for m in range(NJ - 1):
+            arrived(1, m)
+        rest(1)
+
+        @pl.loop(NJ - 1, CX - 1)
+        def _(x):
+            plane(dy.at[it], x, *rows)
+
+        @pl.when(bx > 0)
+        def _():
+            down.wait_send()
+            up.wait_recv()
+
+        @pl.when(bx < NI - 1)
+        def _():
+            up.wait_send()
+            down.wait_recv()
+
+        for x in (0, CX - 1):
+            plane(dy.at[it], x, *rows)
 
         z_planes(0, 1)
         z_planes(CX - 1, 1)
@@ -494,7 +514,7 @@
         def _():
             high.start()
 
-        for x in range(1, CX - 1, 2):
+        for x in range(NJ - 1, CX - 1, 2):
             z_planes(x, 2)
 
         @pl.when(more)
@@ -578,7 +598,7 @@
         c.wait()
     found = [p.astype(BF16) for p in chop(jnp.transpose(got2[...])[:CAP], 3)]
 
-    @pl.loop(0, P_DEV // 256)
+    @pl.loop(0, P_DEV // 256, unroll=4)
     def _(c):
         at = pl.ds(al(c, 256), 256)
         ones = hot(fit(NB, own[:, at]))
@@ -605,11 +625,11 @@
             pltpu.VMEM(tall, F32),
             pltpu.VMEM((2, NI * CX, 128), F32),
             pltpu.VMEM((ITERS, 2, CX, NZ), F32),
-            pltpu.VMEM((ITERS, 2, 2, NJ * CY, 128), F32),
-            pltpu.VMEM((2, 2, NJ * CY, 128), F32),
+            pltpu.VMEM((ITERS, 2, NJ * CY, NZ), F32),
+            pltpu.VMEM((2, NJ * CY, NZ), F32),
             pltpu.VMEM(tall, F32),
             pltpu.VMEM((2, NJ, 8, 128), F32),
-            pltpu.VMEM((ITERS, NJ, 8, NZ), F32),
+            pltpu.VMEM((ITERS, 2, NJ, 8, 128), F32),
             pltpu.VMEM(tall, F32),
             pltpu.VMEM((2, CX, NZ), F32),
             pltpu.VMEM((ITERS, 2, CX, NZ), F32),
@@ -635,7 +655,7 @@
             pltpu.VMEM((NB, 128), F32),
             pltpu.VMEM((NI, NJ, 128), F32),
             pltpu.VMEM((NB, 128), F32),
-            dma((2, NI)), dma((2, NI)), dma((2, NI)), dma((2, NI)),
+            dma((2, NI)), dma((2, NI)), dma((4, NI)), dma((4, NI)),
             dma((2, NI)), dma((2, 2)),
             dma((2, NJ)), dma((2, NJ)), dma((2, NJ)), dma((2, NJ)), dma((2, NJ)), dma((2, NJ)),
             dma((2,)), dma((2,)), dma((4,)), dma((4,)),
@@ -643,7 +663,7 @@
             dma((NJ,)), dma((NJ,)), dma((NI,)), dma((NI,)), dma((3,)),
         ],
         compiler_params=pltpu.CompilerParams(
-            collective_id=0, has_side_effects=True, vmem_limit_bytes=62 << 20
+            collective_id=0, has_side_effects=True, vmem_limit_bytes=61 << 20
         ),
     )(normals, owners.reshape(1, P_DEV), cells.reshape(1, P_DEV), levels, rows, columns, depth)
     return iterate, implicit.reshape(P_DEV)

time: 322 us -> 300 us (0.932)
  Pallas kernels: 317 us -> 296 us
    pallas_call x1, Pallas kernels: 317 us -> 296 us  [local(): pl.pallas_call(relax, name='relax', out_shape=(jax.ShapeDtypeStruct(brick...]
where the time goes in v5:
time: 300 us
  Pallas kernels  296 us (99%)
    pallas_call x1, Pallas kernels, local(): pl.pallas_call(relax, name='relax', out_shape=(jax.ShapeDtypeStruct(brick...  296 us

profile of v5, /device:TPU:1, one launch (start us, length us, event | category | flops | bytes accessed | tf_op | source)
XLA Modules:
  0.0 300.2 jit_solution(16002434253509303417)
XLA Ops:
  1.3 296.0 %relax.1 = (f32[16,64,256]{2,1,0:T(8,128)}, f32[1,4096]{1,0:T(1,128)}) custom-call(f32[3,4096]{1,0:T(4,128)} %nrm.1, s32[1,4096]{1,0:T(1,128)} %bitcast.3, s32[1,4096]{1,0:T(1,128)} %bitcast.4, s32[1,1]{1,0:T(1,128)S(6)} %copy.11.lev_ref, f32[256,256]{1,0:T(8,128)} %mx_ref.1, f32[512,512]{1,0:T(8,128)} %my_ref.1, f32[256,256]{1,0:T(8,128)} %mz_ref.1), custom_call_target="tpu_custom_call" | custom-call | tf_op jit(solution)/shard_map/relax/pallas_call | solution.py:615
  297.3 0.0 copy-start
  297.3 2.3 copy.12
  299.6 0.0 copy-done
  299.6 0.6 copy.13
Async XLA Ops:
  297.3 2.3 copy-start

commit v6 on v5

--- a/solution.py
+++ b/solution.py
@@ -39,6 +39,10 @@
 
 def al(v, m):
     return pl.multiple_of(v * m, m)
+
+
+def held(j):
+    return 4 * (j % 2) + j // 2
 
 
 def greet(bx, by):
@@ -303,14 +307,17 @@
                 es.at[side, 0], er.at[side, z], (bx, by),
             )
 
-        def back(h, part):
+        def back(part, h):
+            low, planes = ((0, 6), (6, 4), (10, 4), (14, 4))[part]
             for t in BX_ORDER:
                 k = bx_peer(bx, t)
-                src = dxp.at[pl.ds(k * 16 + 10 * part, 10 - 2 * part), pl.ds(4 * h, 4)]
-                dst = dx.at[
-                    it, pl.ds(10 * part, 10 - 2 * part), pl.ds(al(2 * yg + h, 4), 4), pl.ds(al(zh, 128), 128)
-                ]
-                n = 2 * part + h
+                if part:
+                    src = dxp.at[pl.ds(k * 16 + low, planes)]
+                    dst = dx.at[it, pl.ds(low, planes), pl.ds(al(yg, 8), 8), pl.ds(al(zh, 128), 128)]
+                else:
+                    src = dxp.at[pl.ds(k * 16, planes), pl.ds(4 * h, 4)]
+                    dst = dx.at[it, pl.ds(0, planes), pl.ds(al(2 * yg + h, 4), 4), pl.ds(al(zh, 128), 128)]
+                n = part + h
                 if t:
                     copies.append(remote(src, dst, bs.at[n, t], br.at[n, t], (k, by)))
                 else:
@@ -329,7 +336,7 @@
                     edge[0] = d[:, :128]
                 if y == 6:
                     edge[1] = d[:, 128:]
-            back(h, 0)
+            back(0, h)
             if h == 0:
 
                 @pl.when((yg == 0) & (by > 0))
@@ -344,8 +351,8 @@
                     for c in edges(1, above):
                         c.start()
 
-        back(0, 1)
-        back(1, 1)
+        for part in range(1, 4):
+            back(part, 1)
         for c in copies[: 2 * NI]:
             c.wait()
 
@@ -359,25 +366,36 @@
             half(1, 0).wait_recv()
             half(1, 1).wait_recv()
 
-        forth = []
-        for e in range(2):
-            if e:
-                for c in copies[2 * NI :]:
+        for part in range(4):
+            if part:
+                for c in copies[NI * (part + 1) : NI * (part + 2)]:
                     c.wait()
-            for t in [*range(1, NJ), 0]:
-                j = (by + t) % NJ
+            e = part // 2
+            for t in (1, 2, 3, 0):
+                i = (by // 2 + t) % 4
+                x, j = 4 * part + i, 2 * i + part % 2
                 plane(
                     dx.at[it],
-                    j + NJ * e,
+                    x,
                     lambda x: yhx[it, 1, pl.ds(x, 1), :],
                     lambda x: yhx[it, 0, pl.ds(x, 1), :],
                 )
-                src, dst = r.at[j + NJ * e], yin.at[it, e, pl.ds(al(by, 64), 64)]
+                src, dst = r.at[x], yin.at[it, e, pl.ds(al(by, 64), 64)]
+
+                def away():
+                    remote(src, dst, ys.at[e, j], yr.at[e, by], (bx, j)).start()
+
                 if t:
-                    forth.append(remote(src, dst, ys.at[e, t], yr.at[e, t], (bx, j)))
+                    away()
                 else:
-                    forth.append(pltpu.make_async_copy(src, dst, ys.at[e, 0]))
-                forth[-1].start()
+                    pl.when(by % 2 != part % 2)(away)
+
+                    @pl.when(by % 2 == part % 2)
+                    def _():
+                        pltpu.make_async_copy(src, dst, yr.at[e, by]).start()
+
+        def gone(e, j):
+            return remote(r.at[0], yin.at[it, e, pl.ds(al(j, 64), 64)], ys.at[e, j], yr.at[e, j], (bx, by))
 
         @pl.when((yg == 0) & (by > 0))
         def _():
@@ -391,8 +409,8 @@
 
         copies = []
         for e in range(2):
-            for c in forth[NJ * e : NJ * (e + 1)]:
-                c.wait()
+            for j in range(NJ):
+                gone(e, j).wait_recv()
             d = dot3(mys[0], mys[1], *split(yin[it, e]))
             dyl[e] = d
             for j in range(NJ):
@@ -403,7 +421,7 @@
                         ye[e, j, 2 + n : 3 + n] = d[64 * j + 64 : 64 * j + 65, 128 * n : 128 * (n + 1)]
             for t in [*range(1, NJ), 0]:
                 j = (by + t) % NJ
-                main = (dyl.at[e, pl.ds(al(j, 64), 64)], dy.at[it, 1 + by + NJ * e])
+                main = (dyl.at[e, pl.ds(al(j, 64), 64)], dy.at[it, 1 + held(by) + NJ * e])
                 outer = (ye.at[e, j], yhy.at[it, e, by])
                 if t:
                     copies.append(remote(*main, cs.at[e, t], cr.at[e, by], (bx, j)))
@@ -414,9 +432,13 @@
                 copies[-2].start()
                 copies[-1].start()
 
+        for t in range(1, NJ):
+            for e in range(2):
+                gone(e, (by + t) % NJ).wait_send()
+
         def arrived(e, m):
             remote(
-                dyl.at[e, pl.ds(0, 64)], dy.at[it, 1 + m + NJ * e], cs.at[e, 0], cr.at[e, m], (bx, by)
+                dyl.at[e, pl.ds(0, 64)], dy.at[it, 1 + held(m) + NJ * e], cs.at[e, 0], cr.at[e, m], (bx, by)
             ).wait_recv()
 
         def rest(e):
@@ -427,7 +449,7 @@
 
         def outer_row(side):
             def load(x):
-                at = (it, x // NJ, x % NJ)
+                at = (it, x // NJ, 2 * (x % 4) + x // 4 % 2)
                 return jnp.concatenate(
                     [yhy[(*at, pl.ds(2 * side + n, 1), slice(None))] for n in range(2)], axis=1
                 )
@@ -655,7 +677,7 @@
             pltpu.VMEM((NB, 128), F32),
             pltpu.VMEM((NI, NJ, 128), F32),
             pltpu.VMEM((NB, 128), F32),
-            dma((2, NI)), dma((2, NI)), dma((4, NI)), dma((4, NI)),
+            dma((2, NI)), dma((2, NI)), dma((5, NI)), dma((5, NI)),
             dma((2, NI)), dma((2, 2)),
             dma((2, NJ)), dma((2, NJ)), dma((2, NJ)), dma((2, NJ)), dma((2, NJ)), dma((2, NJ)),
             dma((2,)), dma((2,)), dma((4,)), dma((4,)),

time: 300 us -> 292 us (0.973)
  Pallas kernels: 296 us -> 288 us
    pallas_call x1, Pallas kernels: 296 us -> 288 us  [local(): pl.pallas_call(relax, name='relax', out_shape=(jax.ShapeDtypeStruct(brick...]
where the time goes in v6:
time: 292 us
  Pallas kernels  288 us (99%)
    pallas_call x1, Pallas kernels, local(): pl.pallas_call(relax, name='relax', out_shape=(jax.ShapeDtypeStruct(brick...  288 us

profile of v6, /device:TPU:1, one launch (start us, length us, event | category | flops | bytes accessed | tf_op | source)
XLA Modules:
  0.0 292.0 jit_solution(8033153111606114498)
XLA Ops:
  1.3 287.8 %relax.1 = (f32[16,64,256]{2,1,0:T(8,128)}, f32[1,4096]{1,0:T(1,128)}) custom-call(f32[3,4096]{1,0:T(4,128)} %nrm.1, s32[1,4096]{1,0:T(1,128)} %bitcast.3, s32[1,4096]{1,0:T(1,128)} %bitcast.4, s32[1,1]{1,0:T(1,128)S(6)} %copy.11.lev_ref, f32[256,256]{1,0:T(8,128)} %mx_ref.1, f32[512,512]{1,0:T(8,128)} %my_ref.1, f32[256,256]{1,0:T(8,128)} %mz_ref.1), custom_call_target="tpu_custom_call" | custom-call | tf_op jit(solution)/shard_map/relax/pallas_call | solution.py:637
  289.1 0.0 copy-start
  289.1 2.3 copy.12
  291.4 0.0 copy-done
  291.4 0.6 copy.13
Async XLA Ops:
  289.1 2.3 copy-start

commit v7 on v6

--- a/solution.py
+++ b/solution.py
@@ -65,7 +65,7 @@
 def relax(
     nrm, own, cel, lev_ref, mx_ref, my_ref, mz_ref, u_ref, imp_ref,
     r, xin, dxp, dx, edge, yhx, yin, dyl, dy, ye, yhy, dz, ze, yhz,
-    mxv, myv, mzv, mxs, mys, mzs,
+    mxv, myv, mzv, mxs, mys, mzs, zpart,
     box, rank, in1, out2, in2, slot, vx, vy, vz, fe, fh, ut, back1, got1, back2, got2,
     xs, xr, bs, br, es, er, ys, yr, cs, cr, ns, nr, hs, hr, zs, zr,
     ps, pr, qs, qr, fs, fr, gs, gr, ks, kr, ms,
@@ -252,11 +252,11 @@
 
     diagonal = 6.0 + (1.0 + lev_ref[0, 0].astype(F32))
 
-    def plane(d, x, low=None, high=None):
+    def plane(d, x, low=None, high=None, under=True):
         c = d[x + 1]
         zi = lax.broadcasted_iota(jnp.int32, (CY, NZ), 1)
         yi = lax.broadcasted_iota(jnp.int32, (CY, NZ), 0)
-        near = d[x] + d[x + 2]
+        near = d[x] + d[x + 2] if under else d[x + 2]
         near = near + jnp.where(zi == 0, 0.0, pltpu.roll(c, 1, 1))
         near = near + jnp.where(zi == NZ - 1, 0.0, pltpu.roll(c, NZ - 1, 1))
         near = near + jnp.where(yi == 0, low(x) if low else 0.0, pltpu.roll(c, 1, 0))
@@ -468,9 +468,12 @@
             arrived(0, m)
         rest(0)
 
+        def z_lines(v):
+            return dot3(*split(v), mzs[0], mzs[1], lanes)
+
         def z_planes(x, n):
             v = r[pl.ds(x, n)].reshape(n * CY, NZ)
-            d = dot3(*split(v), mzs[0], mzs[1], lanes)
+            d = z_lines(v)
             dz[it, pl.ds(x + 1, n)] = d.reshape(n, CY, NZ)
 
         @pl.loop(1, NJ - 1)
@@ -479,6 +482,18 @@
 
         for x in range(1, NJ - 1, 2):
             z_planes(x, 2)
+        plane(dy.at[it], 0, *rows, under=False)
+        zpart[...] = z_lines(r[0])
+        z_down = remote(zpart, dz.at[it, CX + 1], zs.at[0], zr.at[0], (jnp.maximum(bx - 1, 0), by))
+        z_up = remote(dz.at[it, CX], dz.at[it, 0], zs.at[1], zr.at[1], (jnp.minimum(bx + 1, NI - 1), by))
+        low = remote(ze.at[0], yhz.at[it, 0], zs.at[2], zr.at[2], (bx, below))
+        high = remote(ze.at[1], yhz.at[it, 1], zs.at[3], zr.at[3], (bx, above))
+        more = it < ITERS - 1
+
+        @pl.when(more & (bx > 0))
+        def _():
+            z_down.start()
+
         arrived(1, NJ - 1)
 
         @pl.when(bx < NI - 1)
@@ -489,38 +504,35 @@
             arrived(1, m)
         rest(1)
 
+        @pl.when(bx < NI - 1)
+        def _():
+            down.wait_recv()
+
+        plane(dy.at[it], CX - 1, *rows)
+        z_planes(CX - 1, 1)
+
+        @pl.when(more & (bx < NI - 1))
+        def _():
+            z_up.start()
+
         @pl.loop(NJ - 1, CX - 1)
         def _(x):
             plane(dy.at[it], x, *rows)
 
+        for x in range(NJ - 1, CX - 1, 2):
+            z_planes(x, 2)
+
         @pl.when(bx > 0)
         def _():
             down.wait_send()
             up.wait_recv()
+            r[0] += dy[it, 0]
 
         @pl.when(bx < NI - 1)
         def _():
             up.wait_send()
-            down.wait_recv()
-
-        for x in (0, CX - 1):
-            plane(dy.at[it], x, *rows)
 
         z_planes(0, 1)
-        z_planes(CX - 1, 1)
-        down, up = x_planes(dz.at[it], zs, zr)
-        low = remote(ze.at[0], yhz.at[it, 0], zs.at[2], zr.at[2], (bx, below))
-        high = remote(ze.at[1], yhz.at[it, 1], zs.at[3], zr.at[3], (bx, above))
-        more = it < ITERS - 1
-
-        @pl.when(more & (bx > 0))
-        def _():
-            down.start()
-
-        @pl.when(more & (bx < NI - 1))
-        def _():
-            up.start()
-
         outer = jnp.concatenate(
             [r[x, y : y + 1, :] for y in (0, CY - 1) for x in range(CX)], axis=0
         )
@@ -536,9 +548,6 @@
         def _():
             high.start()
 
-        for x in range(NJ - 1, CX - 1, 2):
-            z_planes(x, 2)
-
         @pl.when(more)
         def _():
             @pl.loop(1, CX - 1)
@@ -547,13 +556,14 @@
 
             @pl.when(bx > 0)
             def _():
-                down.wait_send()
-                up.wait_recv()
+                z_down.wait_send()
+                z_up.wait_recv()
 
             @pl.when(bx < NI - 1)
             def _():
-                up.wait_send()
-                down.wait_recv()
+                z_up.wait_send()
+                z_down.wait_recv()
+                dz[it, CX + 1] += z_lines(dy[it, CX])
 
             for x in (0, CX - 1):
                 plane(dz.at[it], x)
@@ -661,6 +671,7 @@
             pltpu.VMEM((2, 256, 256), BF16),
             pltpu.VMEM((2, 512, 512), BF16),
             pltpu.VMEM((2, 256, 256), BF16),
+            pltpu.VMEM((CY, NZ), F32),
             pltpu.VMEM((2, NB, 128), F32),
             pltpu.VMEM((1, P_DEV), jnp.int32),
             pltpu.VMEM((2, NB, 128), F32),

time: 292 us -> 289 us (0.990)
  Pallas kernels: 288 us -> 285 us
where the time goes in v7:
time: 289 us
  Pallas kernels  285 us (99%)
  local copies, waits for them, and re-layouts  2.91 us (1%)
    pallas_call x1, Pallas kernels, local(): pl.pallas_call(relax, name='relax', out_shape=(jax.ShapeDtypeStruct(brick...  285 us

profile of v7, /device:TPU:1, one launch (start us, length us, event | category | flops | bytes accessed | tf_op | source)
XLA Modules:
  0.0 289.2 jit_solution(13979168513530825696)
XLA Ops:
  1.3 285.0 %relax.1 = (f32[16,64,256]{2,1,0:T(8,128)}, f32[1,4096]{1,0:T(1,128)}) custom-call(f32[3,4096]{1,0:T(4,128)} %nrm.1, s32[1,4096]{1,0:T(1,128)} %bitcast.3, s32[1,4096]{1,0:T(1,128)} %bitcast.4, s32[1,1]{1,0:T(1,128)S(6)} %copy.11.lev_ref, f32[256,256]{1,0:T(8,128)} %mx_ref.1, f32[512,512]{1,0:T(8,128)} %my_ref.1, f32[256,256]{1,0:T(8,128)} %mz_ref.1), custom_call_target="tpu_custom_call" | custom-call | tf_op jit(solution)/shard_map/relax/pallas_call | solution.py:647
  286.3 0.0 copy-start
  286.3 2.3 copy.12
  288.6 0.0 copy-done
  288.6 0.6 copy.13
Async XLA Ops:
  286.3 2.3 copy-start

commit v8 on v7

--- a/solution.py
+++ b/solution.py
@@ -139,7 +139,7 @@
 
     all_here()
     copies = []
-    for t in range(NI):
+    for t in BX_ORDER:
         k = bx_peer(bx, t)
         src, dst = box.at[:, pl.ds(al(k, 8), 8)], in1.at[:, pl.ds(al(bx, 8), 8)]
         if t:
@@ -397,16 +397,6 @@
         def gone(e, j):
             return remote(r.at[0], yin.at[it, e, pl.ds(al(j, 64), 64)], ys.at[e, j], yr.at[e, j], (bx, by))
 
-        @pl.when((yg == 0) & (by > 0))
-        def _():
-            for c in edges(0, below):
-                c.wait_send()
-
-        @pl.when((yg == 7) & (by < NJ - 1))
-        def _():
-            for c in edges(1, above):
-                c.wait_send()
-
         copies = []
         for e in range(2):
             for j in range(NJ):
@@ -436,15 +426,24 @@
             for e in range(2):
                 gone(e, (by + t) % NJ).wait_send()
 
+        @pl.when((yg == 0) & (by > 0))
+        def _():
+            for c in edges(0, below):
+                c.wait_send()
+
+        @pl.when((yg == 7) & (by < NJ - 1))
+        def _():
+            for c in edges(1, above):
+                c.wait_send()
+
         def arrived(e, m):
             remote(
                 dyl.at[e, pl.ds(0, 64)], dy.at[it, 1 + held(m) + NJ * e], cs.at[e, 0], cr.at[e, m], (bx, by)
             ).wait_recv()
 
         def rest(e):
-            for n in range(2 * NJ * e, 2 * NJ * (e + 1) - 2, 2):
-                copies[n].wait_send()
-                copies[n + 1].wait()
+            for n in range(2 * NJ * e + 1, 2 * NJ * (e + 1) - 1, 2):
+                copies[n].wait_recv()
             copies[2 * NJ * (e + 1) - 1].wait()
 
         def outer_row(side):
@@ -548,6 +547,10 @@
         def _():
             high.start()
 
+        for e in range(2):
+            for n in range(2 * NJ * e, 2 * NJ * (e + 1) - 2):
+                copies[n].wait_send()
+
         @pl.when(more)
         def _():
             @pl.loop(1, CX - 1)
@@ -618,7 +621,7 @@
     for k in range(NI):
         back2[k] = got1[pl.ds(k, NJ, stride=NI), :]
     copies = []
-    for t in range(NI):
+    for t in BX_ORDER:
         k = bx_peer(bx, t)
         src, dst = back2.at[k], got2.at[pl.ds(al(bx, 8), 8)]
         if t:

time: 289 us -> 290 us (level)
  no operation moved by 1% of the time
where the time goes in v8:
time: 290 us
  Pallas kernels  286 us (99%)
  local copies, waits for them, and re-layouts  2.91 us (1%)
    pallas_call x1, Pallas kernels, local(): pl.pallas_call(relax, name='relax', out_shape=(jax.ShapeDtypeStruct(brick...  286 us

profile of v8, /device:TPU:1, one launch (start us, length us, event | category | flops | bytes accessed | tf_op | source)
XLA Modules:
  0.0 289.9 jit_solution(10925561544586697180)
XLA Ops:
  1.3 285.7 %relax.1 = (f32[16,64,256]{2,1,0:T(8,128)}, f32[1,4096]{1,0:T(1,128)}) custom-call(f32[3,4096]{1,0:T(4,128)} %nrm.1, s32[1,4096]{1,0:T(1,128)} %bitcast.3, s32[1,4096]{1,0:T(1,128)} %bitcast.4, s32[1,1]{1,0:T(1,128)S(6)} %copy.11.lev_ref, f32[256,256]{1,0:T(8,128)} %mx_ref.1, f32[512,512]{1,0:T(8,128)} %my_ref.1, f32[256,256]{1,0:T(8,128)} %mz_ref.1), custom_call_target="tpu_custom_call" | custom-call | tf_op jit(solution)/shard_map/relax/pallas_call | solution.py:650
  287.0 0.0 copy-start
  287.0 2.3 copy.12
  289.3 0.0 copy-done
  289.3 0.6 copy.13
Async XLA Ops:
  287.0 2.3 copy-start
